TPU v7x, 32 devices: a whole 2x2x4 slice. The times are simulated.
32 devices in a mesh: facet: 4 (over z), col: 8 (over y, x, core).
Axes of the slice: x: 2, y: 2, z: 4, core: 2. Of those that a mesh axis runs over, the one named last changes fastest.
Arguments:
- facets: bfloat16 [4, 64, 2, 128], P('facet', 'col'), may hold values from -6 to 6
- sub_offsets: int32 [8, 4], P('col'), may hold values from 0 to 8191
- col_offsets: int32 [8], P('col'), may hold values from 0 to 8191
- screen_index: int32 [8, 4], P('col', 'facet'), may hold values from 0 to 3
- screens: float32 [4, 2, 256, 256], replicated, may hold values from -6 to 6
Outputs:
- facets_out: float32 [4, 64, 2, 128], P('facet', 'col')
All inputs are finite; a program needn't handle non-finite values.
Results may differ from a plain program's by a relative error of at most 0.0056.
Values may be sent and summed in bfloat16 or wider, within the bound.
No kernel may reach another device: no remote copies, remote signals or barrier semaphores. Data moves between devices by JAX's collectives and lax.ppermute only.
A program may use at most 64 MiB of HBM per device.

v0:
```python
import math

import jax
import jax.numpy as jnp
from jax import lax
from jax.sharding import PartitionSpec as P

XC = 64
XS = 256
SLAB = 128
NPAD = 8192


def phase_pair(numerator, period, direction, factor):
    angles = direction * 2.0 * math.pi / period * numerator.astype(jnp.float32)
    return (
        (jnp.cos(angles) * factor).astype(jnp.bfloat16),
        (jnp.sin(angles) * factor).astype(jnp.bfloat16),
    )


def embed_table(facet_ids):
    column = jnp.arange(XS, dtype=jnp.int32)
    within = jnp.arange(XC, dtype=jnp.int32)
    product = column[None, :, None] * (within[None, None, :] + 7 * facet_ids[:, None, None]) % XS
    return phase_pair(product, XS, 1.0, 1.0 / math.sqrt(XS))


def column_table(offset):
    position = jnp.arange(SLAB, dtype=jnp.int32)
    frequency = (offset + jnp.arange(XC, dtype=jnp.int32)) % NPAD
    product = position[:, None] * frequency[None, :] % NPAD
    return phase_pair(product, NPAD, -1.0, 1.0 / math.sqrt(SLAB))


def row_table(offsets, row_ids, height):
    frequency = (offsets[:, None] + jnp.arange(XC, dtype=jnp.int32)[None, :]) % NPAD
    frequency = frequency.reshape(frequency.shape + (1,) * row_ids.ndim)
    product = frequency * (row_ids % NPAD) % NPAD
    return phase_pair(product, NPAD, -1.0, 1.0 / math.sqrt(height))


def general_dot(first_op, second_op, contract):
    numbers = ((contract[0], contract[1]), ((), ()))
    return lax.dot_general(first_op, second_op, numbers, preferred_element_type=jnp.float32)


def complex_dot(first_op, second_op, contract):
    real_part = general_dot(first_op[0], second_op[0], contract) - general_dot(
        first_op[1], second_op[1], contract
    )
    imag_part = general_dot(first_op[0], second_op[1], contract) + general_dot(
        first_op[1], second_op[0], contract
    )
    return (real_part, imag_part)


def complex_einsum(form, first_op, second_op):

    def single(left_part, right_part):
        return jnp.einsum(form, left_part, right_part, preferred_element_type=jnp.float32)

    real_part = single(first_op[0], second_op[0]) - single(first_op[1], second_op[1])
    imag_part = single(first_op[0], second_op[1]) + single(first_op[1], second_op[0])
    return (real_part, imag_part)


def round_pair(values):
    return (values[0].astype(jnp.bfloat16), values[1].astype(jnp.bfloat16))


def body(facets, sub_offsets, col_offsets, screen_index, screens):
    facet_now = lax.axis_index("facet")
    facet_count = lax.axis_size("facet")
    column_count = lax.axis_size("col")
    local_rows = facets.shape[1]
    total_rows = local_rows * column_count
    subgrid_count = sub_offsets.shape[1]
    across = column_table(col_offsets[0])
    row_ids = facet_now * total_rows + jnp.arange(total_rows, dtype=jnp.int32)
    row_phase = row_table(sub_offsets[0], row_ids, total_rows)
    row_flat = (
        row_phase[0].reshape(subgrid_count * XC, total_rows),
        row_phase[1].reshape(subgrid_count * XC, total_rows),
    )
    embedding = embed_table(jnp.arange(facet_count, dtype=jnp.int32))
    adjoint_embed = (embedding[0], -embedding[1])
    whole_slab = lax.all_gather(facets[0], "col", axis=0, tiled=True)
    spread = round_pair(complex_dot((whole_slab[:, 0], whole_slab[:, 1]), across, ((1,), (0,))))
    block_phase = (row_flat[0], row_flat[1])
    summand = complex_dot(block_phase, spread, ((1,), (0,)))
    contrib_real = summand[0]
    contrib_imag = summand[1]
    contributions = jnp.stack(
        [contrib_real.reshape(subgrid_count, XC, XC), contrib_imag.reshape(subgrid_count, XC, XC)],
        axis=1,
    ).astype(jnp.bfloat16)
    outgoing = contributions.reshape(facet_count, subgrid_count // facet_count, 2, XC, XC)
    received = lax.all_to_all(outgoing, "facet", split_axis=0, concat_axis=0, tiled=True)
    factor = 1.0 / math.sqrt(received.shape[0])
    halfway = round_pair(
        complex_einsum("fkuv,fav->fkua", (received[:, :, 0], received[:, :, 1]), embedding)
    )
    subgrid = complex_einsum("fau,fkub->kab", embedding, halfway)
    subgrids = jnp.stack([subgrid[0] * factor, subgrid[1] * factor], axis=1)
    gain_maps = jnp.take(screens, screen_index[0], axis=0)
    sub_real = subgrids[:, 0]
    sub_imag = subgrids[:, 1]
    gain_real = gain_maps[:, 0]
    gain_imag = gain_maps[:, 1]
    screened = jnp.stack(
        [sub_real * gain_real - sub_imag * gain_imag, sub_real * gain_imag + sub_imag * gain_real],
        axis=1,
    ).astype(jnp.bfloat16)
    inner = round_pair(
        complex_einsum("fau,kab->fkub", adjoint_embed, (screened[:, 0], screened[:, 1]))
    )
    returned = round_pair(complex_einsum("fkub,fbv->fkuv", inner, adjoint_embed))
    going_back = jnp.stack([returned[0], returned[1]], axis=2)
    arrived = lax.all_to_all(going_back, "facet", split_axis=0, concat_axis=0, tiled=True)
    flat_parts = (
        arrived[:, :, 0].reshape(subgrid_count * XC, XC),
        arrived[:, :, 1].reshape(subgrid_count * XC, XC),
    )
    conj_rows = (row_flat[0], -row_flat[1])
    conj_across = (across[0], -across[1])
    block_phase = (conj_rows[0], conj_rows[1])
    slab_rows = round_pair(complex_dot(block_phase, flat_parts, ((0,), (0,))))
    summand = complex_dot(slab_rows, conj_across, ((1,), (1,)))
    summed = lax.psum_scatter(
        jnp.stack([summand[0], summand[1]], axis=1), "col", scatter_dimension=0, tiled=True
    )
    factor = 1.0 / math.sqrt(column_count * subgrid_count)
    return (summed * factor)[None]


def solution(mesh):
    return jax.shard_map(
        body,
        mesh=mesh,
        in_specs=(P("facet", "col", None, None), P("col", None), P("col"), P("col", "facet"), P()),
        out_specs=P("facet", "col", None, None),
        check_vma=False,
    )
```

profile of v0, /device:TPU:0, one launch (start us, length us, event | category | flops | bytes accessed | tf_op | source)
XLA Modules:
  0.0 103.0 jit_solution(15256467704068832730)
XLA Ops:
  6.5 0.0 copy-start
  7.4 0.7 copy.23
  8.0 10.3 %all-gather = bf16[1,64,2,128]{3,1,2,0:T(8,128)(2,1)S(1)} all-gather(bf16[1,8,2,128]{3,1,2,0:T(8,128)(2,1)S(1)} %copy.23), channel_id=2, replica_groups=mesh['facet'=4,'col'=8] {'col'}, dimensions={1}, use_global_device_ids=true | all-gather | bytes 36864 | tf_op jit(solution)/shard_map/all_gather | solution.py:88
  18.4 0.4 fusion.56
  18.8 0.4 fusion.54
  19.2 0.4 fusion.17
  19.7 0.7 iota_add_fusion.1
  20.4 0.1 add.272
  20.5 0.4 fusion.16
  20.9 0.7 fusion.47
  21.6 0.7 fusion.48
  22.3 0.7 fusion.13
  23.0 0.1 copy.40
  23.1 0.7 fusion.12
  23.8 0.1 copy.39
  24.0 0.8 reshape.305
  24.8 4.9 %all-to-all-start = ((bf16[4,2,4096]{2,1,0:T(2,128)(2,1)}), bf16[4,2,4096]{2,1,0:T(2,128)(2,1)S(1)}, u32[]{:S(2)}, u32[]{:S(2)}) async-start(bf16[4,2,4096]{2,1,0:T(2,128)(2,1)} %reshape.305), calls=%async_computation | async-start | bytes 131072 | tf_op jit(solution)/shard_map/all_to_all | solution.py:99
  29.6 0.0 reduce-scatter.2.cloned.1.call-start
  30.3 0.0 copy-done
  30.4 0.2 copy.43
  30.6 0.1 iota_add_fusion
  30.7 1.1 %multiply_convert_fusion.1 = bf16[4,256,64]{1,2,0:T(8,128)(2,1)S(1)} fusion(s32[4,64]{1,0:T(4,128)S(1)} %iota_add_fusion), kind=kLoop, calls=%fused_computation.50 | loop fusion | flops 1048576 | bytes 132096 | tf_op jit(solution)/shard_map/convert_element_type | solution.py:17
  31.8 1.1 %fusion.33 = bf16[4,256,64]{1,2,0:T(8,128)(2,1)S(1)} fusion(s32[4,64]{1,0:T(4,128)S(1)} %iota_add_fusion), kind=kLoop, calls=%fused_computation.68 | loop fusion | flops 1245184 | bytes 132096 | tf_op jit(solution)/shard_map/neg | solution.py:87
  32.8 2.5 %all-to-all-done = bf16[4,2,4096]{2,1,0:T(2,128)(2,1)S(1)} async-done(((bf16[4,2,4096]{2,1,0:T(2,128)(2,1)}), bf16[4,2,4096]{2,1,0:T(2,128)(2,1)S(1)}, u32[]{:S(2)}, u32[]{:S(2)}) %all-to-all-start) | async-done | bytes 65568 | tf_op jit(solution)/shard_map/all_to_all | solution.py:99
  35.4 0.1 reshape.306
  35.5 1.6 %fusion.34 = f32[4,64,256]{2,1,0:T(8,128)S(1)} fusion(s32[4,64]{1,0:T(4,128)S(1)} %iota_add_fusion, bf16[4,1,2,64,64]{4,3,2,1,0:T(8,128)(2,1)S(1)} %reshape.306), kind=kOutput, calls=%fused_computation.69 | convolution fusion | flops 9437184 | bytes 329728 | tf_op jit(solution)/shard_map/fkuv,fav->fkua/dot_general | solution.py:61
  37.2 1.4 %fusion.36 = f32[4,64,256]{2,1,0:T(8,128)S(1)} fusion(s32[4,64]{1,0:T(4,128)S(1)} %iota_add_fusion, bf16[4,1,2,64,64]{4,3,2,1,0:T(8,128)(2,1)S(1)} %reshape.306), kind=kOutput, calls=%fused_computation.71 | convolution fusion | flops 9437184 | bytes 329728 | tf_op jit(solution)/shard_map/fkuv,fav->fkua/dot_general | solution.py:61
  38.6 1.2 %fusion.7 = bf16[4,64,256]{2,1,0:T(8,128)(2,1)S(1)} fusion(f32[4,64,256]{2,1,0:T(8,128)S(1)} %fusion.34, s32[4,64]{1,0:T(4,128)S(1)} %iota_add_fusion, bf16[4,1,2,64,64]{4,3,2,1,0:T(8,128)(2,1)S(1)} %reshape.306), kind=kOutput, calls=%fused_computation.13 | convolution fusion | flops 9568256 | bytes 460800 | tf_op jit(solution)/shard_map/fkuv,fav->fkua/dot_general | solution.py:61
  39.8 1.2 %convolution_bitcast_fusion.2 = f32[256,256]{1,0:T(8,128)S(1)} fusion(bf16[4,64,256]{2,1,0:T(8,128)(2,1)S(1)} %fusion.7, s32[4,64]{1,0:T(4,128)S(1)} %iota_add_fusion), kind=kOutput, calls=%fused_computation.4 | convolution fusion | flops 34603008 | bytes 394240 | tf_op jit(solution)/shard_map/fau,fkub->kab/dot_general | solution.py:61
  41.0 1.2 %fusion.6 = bf16[4,64,256]{2,1,0:T(8,128)(2,1)S(1)} fusion(f32[4,64,256]{2,1,0:T(8,128)S(1)} %fusion.36, s32[4,64]{1,0:T(4,128)S(1)} %iota_add_fusion, bf16[4,1,2,64,64]{4,3,2,1,0:T(8,128)(2,1)S(1)} %reshape.306), kind=kOutput, calls=%fused_computation.12 | convolution fusion | flops 9568256 | bytes 460800 | tf_op jit(solution)/shard_map/fkuv,fav->fkua/dot_general | solution.py:61
  42.2 1.2 %convolution_bitcast_fusion = f32[256,256]{1,0:T(8,128)S(1)} fusion(bf16[4,64,256]{2,1,0:T(8,128)(2,1)S(1)} %fusion.6, s32[4,64]{1,0:T(4,128)S(1)} %iota_add_fusion), kind=kOutput, calls=%fused_computation.2 | convolution fusion | flops 34603008 | bytes 394240 | tf_op jit(solution)/shard_map/fau,fkub->kab/dot_general | solution.py:61
  43.4 1.2 %fusion.2 = f32[1,256,256]{1,2,0:T(8,128)S(1)} fusion(f32[256,256]{1,0:T(8,128)S(1)} %convolution_bitcast_fusion.2, bf16[4,64,256]{2,1,0:T(8,128)(2,1)S(1)} %fusion.6, s32[4,64]{1,0:T(4,128)S(1)} %iota_add_fusion), kind=kOutput, calls=%fused_computation.8 | convolution fusion | flops 34734080 | bytes 656384 | tf_op jit(solution)/shard_map/fau,fkub->kab/dot_general | solution.py:61
  44.6 1.2 %fusion.30 = (bf16[256,256]{0,1:T(8,128)(2,1)S(1)}, bf16[256,256]{0,1:T(8,128)(2,1)S(1)}) fusion(f32[1,2,256,256]{2,3,1,0:T(8,128)S(1)} %broadcast_select_fusion, f32[1,256,256]{1,2,0:T(8,128)S(1)} %fusion.2, f32[256,256]{1,0:T(8,128)S(1)} %convolution_bitcast_fusion, bf16[4,64,256]{2,1,0:T(8,128)(2,1)S(1)} %fusion.7, s32[4,64]{1,0:T(4,128)S(1)} %iota_add_fusion), kind=kOutput, calls=%fused_computation.63 | convolution fusion | flops 35258368 | bytes 1442816 | tf_op jit(solution)/shard_map/fau,fkub->kab/dot_general | solution.py:61
  45.8 0.2 fusion.204
  46.1 0.2 fusion.206
  46.3 0.2 fusion.205
  46.5 0.2 fusion.207
  46.8 1.4 %fusion.38 = f32[4,64,64]{2,1,0:T(8,128)S(1)} fusion(bf16[4,64,256]{2,1,0:T(8,128)(2,1)S(1)} %fusion.31, s32[4,64]{1,0:T(4,128)S(1)} %iota_add_fusion), kind=kOutput, calls=%fused_computation.77 | convolution fusion | flops 9633792 | bytes 197632 | tf_op jit(solution)/shard_map/fkub,fbv->fkuv/dot_general | solution.py:61
  48.2 1.4 %fusion.35 = f32[4,64,64]{2,1,0:T(8,128)S(1)} fusion(bf16[4,64,256]{2,1,0:T(8,128)(2,1)S(1)} %fusion.31, s32[4,64]{1,0:T(4,128)S(1)} %iota_add_fusion), kind=kOutput, calls=%fused_computation.70 | convolution fusion | flops 9437184 | bytes 197632 | tf_op jit(solution)/shard_map/fkub,fbv->fkuv/dot_general | solution.py:61
  49.6 0.1 fusion.32
  49.7 1.2 %fusion.10 = bf16[4,1,1,64,64]{4,3,0,2,1:T(8,128)(2,1)S(1)} fusion(f32[4,64,64]{2,1,0:T(8,128)S(1)} %fusion.38, bf16[4,64,256]{2,1,0:T(8,128)(2,1)S(1)} %fusion.32, s32[4,64]{1,0:T(4,128)S(1)} %iota_add_fusion), kind=kOutput, calls=%fused_computation.20 | convolution fusion | flops 9469952 | bytes 230400 | tf_op jit(solution)/shard_map/fkub,fbv->fkuv/dot_general | solution.py:61
  50.9 1.2 %fusion.11 = bf16[4,1,1,64,64]{4,3,0,2,1:T(8,128)(2,1)S(1)} fusion(f32[4,64,64]{2,1,0:T(8,128)S(1)} %fusion.35, bf16[4,64,256]{2,1,0:T(8,128)(2,1)S(1)} %fusion.32, s32[4,64]{1,0:T(4,128)S(1)} %iota_add_fusion), kind=kOutput, calls=%fused_computation.21 | convolution fusion | flops 9666560 | bytes 230400 | tf_op jit(solution)/shard_map/fkub,fbv->fkuv/dot_general | solution.py:61
  52.1 0.2 reshape.307
  52.3 8.1 %all_to_all.10 = bf16[4,2,4096]{2,1,0:T(2,128)(2,1)S(1)} all-to-all(bf16[4,2,4096]{2,1,0:T(2,128)(2,1)S(1)} %reshape.307), channel_id=1, replica_groups=mesh['facet'=4,'col'=8] {'facet'}, dimensions={0} | all-to-all | bytes 131072 | tf_op jit(solution)/shard_map/all_to_all | solution.py:120
  60.4 0.1 reshape.308
  60.5 0.7 fusion.46
  61.3 0.7 fusion.45
  62.0 0.7 fusion.18
  62.7 0.4 fusion.57
  63.1 0.4 fusion.53
  63.5 0.7 fusion.19
  64.3 0.4 fusion.14
  64.6 0.4 fusion.15
  65.0 0.6 pad_maximum_fusion.2
  65.7 0.0 reduce-scatter.2.cloned.1.call-update
  65.7 29.2 %reduce-scatter.2.cloned.1.call-done = f32[8,2,128]{2,0,1:T(8,128)} async-done(((f32[64,2,128]{2,0,1:T(8,128)}), f32[8,2,128]{2,0,1:T(8,128)}) %reduce-scatter.2.cloned.1.call-update) | async-done | bytes 8208 | tf_op jit(solution)/shard_map/reduce_scatter | solution.py:130
  94.8 0.7 multiply_bitcast_fusion
  95.5 0.6 copy.34
  (11 shorter events, 0.2 us)
Async XLA Ops:
  6.5 23.8 %copy-start = (f32[4,2,256,256]{3,2,1,0:T(8,128)S(1)}, f32[4,2,256,256]{3,2,1,0:T(8,128)}, u32[]{:S(2)}) copy-start(f32[4,2,256,256]{3,2,1,0:T(8,128)} %param.9) | copy-start | bytes 6291460
  24.8 10.6 %all-to-all-start = ((bf16[4,2,4096]{2,1,0:T(2,128)(2,1)}), bf16[4,2,4096]{2,1,0:T(2,128)(2,1)S(1)}, u32[]{:S(2)}, u32[]{:S(2)}) async-start(bf16[4,2,4096]{2,1,0:T(2,128)(2,1)} %reshape.305), calls=%async_computation | async-start | bytes 131072 | tf_op jit(solution)/shard_map/all_to_all | solution.py:99
  29.6 65.2 %reduce-scatter.2.cloned.1.call-start = ((), (), s32[]{:S(2)}) async-start(), calls=%async_computation.3 | async-start | bytes 73728 | tf_op jit(solution)/shard_map/reduce_scatter | solution.py:130
Sparse Core Ops, SparseCore 0:
  65.8 28.9 reduce-scatter.1
where the time goes:
time: 103 us
  waiting for transfers between devices  31.7 us (31%)
  matrix products  25.2 us (24%)
  blocking collectives  18.4 us (18%)
  between operations  15.1 us (15%)
  starting transfers between devices  4.87 us (5%)
  other arithmetic  4.49 us (4%)
  local copies, waits for them, and re-layouts  3.13 us (3%)
    reduce_scatter x1, waiting for transfers between devices, body(): lax.psum_scatter(jnp.stack([summand[0], summand[1]], axis=1), 'col', scat...  29.2 us
    dot_general x12, matrix products, single(): jnp.einsum(form, left_part, right_part, preferred_element_type=jnp.float32)  15.4 us
    all_gather x1, blocking collectives, body(): whole_slab = lax.all_gather(facets[0], 'col', axis=0, tiled=True)  10.3 us
    dot_general x16, matrix products, general_dot(): lax.dot_general(first_op, second_op, numbers, preferred_element_type=jnp....  8.9 us
    all_to_all x1, blocking collectives, body(): lax.all_to_all(going_back, 'facet', split_axis=0, concat_axis=0, tiled=True)  8.11 us
    all_to_all x1, starting transfers between devices, body(): lax.all_to_all(outgoing, 'facet', split_axis=0, concat_axis=0, tiled=True)  4.87 us
    all_to_all x1, waiting for transfers between devices, body(): lax.all_to_all(outgoing, 'facet', split_axis=0, concat_axis=0, tiled=True)  2.54 us
    unnamed x8, local copies, waits for them, and re-layouts  2.12 us
  transfers between devices with their start and end apart: 2, of which 2 were waited for; matrix products, arithmetic and copies ran while one was open for 2% of the time, Pallas kernels for 0%

commit v1 on v0

v1 whole, which is shorter than its diff:
```python
import functools
import math

import jax
import jax.numpy as jnp
from jax import lax
from jax.experimental import pallas as pl
from jax.experimental.pallas import tpu as pltpu
from jax.sharding import PartitionSpec as P

XC = 64
NPAD = 8192
STEP = 7
LANES = 128
CHUNK = 256
F32 = jnp.float32
BF16 = jnp.bfloat16
VMEM = pltpu.MemorySpace.VMEM


def wave(number, period, scale):
    quarter = period // 4
    bits = quarter.bit_length() - 1
    turn = (number + quarter // 2) >> bits
    angle = (number - (turn << bits)).astype(F32) * (2.0 * math.pi / period)
    square = angle * angle
    sine = angle * (1.0 + square * (-1 / 6 + square * (1 / 120 + square * (-1 / 5040))))
    cosine = 1.0 + square * (-1 / 2 + square * (1 / 24 + square * (-1 / 720 + square * (1 / 40320))))
    odd = (turn & 1) == 1
    first = jnp.where(odd, sine, cosine)
    second = jnp.where(odd, cosine, sine)
    first = jnp.where(((turn + 1) & 2) == 2, -scale, scale) * first
    second = jnp.where((turn & 2) == 2, -scale, scale) * second
    return first, second


def each(count, step):
    if count == 1:
        step(0)
    else:
        lax.fori_loop(0, count, lambda i, c: (step(i), c)[1], 0)


def iota(shape, axis):
    return lax.broadcasted_iota(jnp.int32, shape, axis)


def tables_kernel(
    dims, col_ref, sub_ref, pick_ref, screens_ref,
    a_ref, p_ref, w_ref, wt_ref, wc_ref, wh_ref, ph_ref, ah_ref, gain_ref, sem,
):
    facets, height, span, slab, size, owned, chunk = dims
    rows = facets * height
    copies = [
        pltpu.make_async_copy(screens_ref.at[pick_ref[k]], gain_ref.at[k], sem.at[k])
        for k in range(owned)
    ]
    for copy in copies:
        copy.start()
    shift = height.bit_length() - 1

    def phases(p, row, offset):
        u = p - STEP * (row >> shift)
        frequency = (offset + u) & (NPAD - 1)
        number = (frequency * (row & (NPAD - 1))) & (NPAD - 1)
        inside = (u >= 0) & (u < XC)
        real, imag = wave(number, NPAD, 1.0 / math.sqrt(height))
        zero = jnp.zeros_like(real)
        return jnp.where(inside, real, zero).astype(BF16), jnp.where(inside, -imag, zero).astype(BF16)

    def row_chunk(k, i):
        base = i * chunk
        along = pl.ds(pl.multiple_of(base, chunk), chunk) if not isinstance(i, int) else pl.ds(base, chunk)
        shape = (span, chunk)
        real, imag = phases(iota(shape, 0), iota(shape, 1) + base, sub_ref[k])
        p_ref[k, :span, along] = real
        p_ref[k, span:, along] = imag
        shape = (chunk, span)
        real, imag = phases(iota(shape, 1), iota(shape, 0) + base, sub_ref[k])
        ph_ref[k, along, :span] = real
        ph_ref[k, along, span:] = imag

    for k in range(owned):
        each(rows // chunk, functools.partial(row_chunk, k))

    def across(x, v):
        frequency = (col_ref[0] + v) & (NPAD - 1)
        number = (x * frequency) & (NPAD - 1)
        real, imag = wave(number, NPAD, 1.0 / math.sqrt(slab))
        zero = jnp.zeros_like(real)
        inside = v < XC
        return jnp.where(inside, real, zero).astype(BF16), jnp.where(inside, -imag, zero).astype(BF16)

    shape = (slab, span)
    real, imag = across(iota(shape, 0), iota(shape, 1))
    a_ref[:slab, :span] = real
    a_ref[:slab, span:] = imag
    a_ref[slab:, :span] = -imag
    a_ref[slab:, span:] = real
    shape = (span, slab)
    real, imag = across(iota(shape, 1), iota(shape, 0))
    ah_ref[:span, :slab] = real
    ah_ref[:span, slab:] = -imag
    ah_ref[span:, :slab] = imag
    ah_ref[span:, slab:] = real

    scale = 1.0 / math.sqrt(size)
    shape = (size, span)
    real, imag = wave((iota(shape, 0) * iota(shape, 1)) & (size - 1), size, scale)
    real, imag = real.astype(BF16), imag.astype(BF16)
    w_ref[:, :span] = real
    w_ref[:, span:] = imag
    wc_ref[:size, :span] = real
    wc_ref[:size, span:] = -imag
    wc_ref[size:, :span] = imag
    wc_ref[size:, span:] = real
    shape = (span, size)
    real, imag = wave((iota(shape, 0) * iota(shape, 1)) & (size - 1), size, scale)
    wh_ref[:span, :] = real.astype(BF16)
    wh_ref[span:, :] = imag.astype(BF16)
    factor = 1.0 / math.sqrt(facets)
    real, imag = (real * factor).astype(BF16), (imag * factor).astype(BF16)
    wt_ref[:span, :size] = real
    wt_ref[:span, size:] = imag
    wt_ref[span:, :size] = -imag
    wt_ref[span:, size:] = real
    for copy in copies:
        copy.wait()


def dot(first, second):
    return jnp.dot(first, second, preferred_element_type=F32)


def main_kernel(
    dims, x_ref, a_ref, p_ref, w_ref, wt_ref, wc_ref, wh_ref, ph_ref, ah_ref, gain_ref, out_ref,
    spread_ref,
):
    facets, height, span, slab, size, owned, chunk = dims
    rows = facets * height

    def turned(block, base, sign):
        parts = []
        for i in range(block.shape[0] // height):
            amount = STEP * (base + i)
            if isinstance(amount, int) and amount == 0:
                parts.append(block[i * height : (i + 1) * height].astype(BF16))
                continue
            amount = amount if sign > 0 else span - amount
            piece = block[i * height : (i + 1) * height]
            halves = [pltpu.roll(piece[:, h * span : (h + 1) * span], amount, 1) for h in (0, 1)]
            parts.append(jnp.concatenate(halves, axis=1).astype(BF16))
        return parts[0] if len(parts) == 1 else jnp.concatenate(parts, axis=0)

    def along(i):
        return pl.ds(i * chunk, chunk) if isinstance(i, int) else pl.ds(pl.multiple_of(i * chunk, chunk), chunk)

    def spread(i):
        block = dot(x_ref[along(i), :], a_ref[...])
        spread_ref[along(i), :] = turned(block, i * (chunk // height), 1)

    each(rows // chunk, spread)
    total = []
    for k in range(owned):
        quad = dot(p_ref[k], spread_ref[...])
        real = (quad[:span, :span] - quad[span:, span:]).astype(BF16)
        imag = (quad[:span, span:] + quad[span:, :span]).astype(BF16)
        both = jnp.concatenate(
            [jnp.concatenate([real, imag], axis=1), jnp.concatenate([-imag, real], axis=1)], axis=0
        )
        half = dot(w_ref[...], both).astype(BF16)
        grid = dot(half, wt_ref[...])
        real, imag = grid[:, :size], grid[:, size:]
        gain_real, gain_imag = gain_ref[k, 0], gain_ref[k, 1]
        seen = jnp.concatenate(
            [
                (real * gain_real - imag * gain_imag).astype(BF16),
                (real * gain_imag + imag * gain_real).astype(BF16),
            ],
            axis=1,
        )
        inner = dot(seen, wc_ref[...]).astype(BF16)
        quad = dot(wh_ref[...], inner)
        real = (quad[:span, :span] + quad[span:, span:]).astype(BF16)
        imag = (quad[:span, span:] - quad[span:, :span]).astype(BF16)
        total.append(
            jnp.concatenate(
                [jnp.concatenate([real, imag], axis=1), jnp.concatenate([imag, -real], axis=1)], axis=0
            )
        )

    def back(i):
        block = dot(ph_ref[0, along(i), :], total[0])
        for k in range(1, owned):
            block += dot(ph_ref[k, along(i), :], total[k])
        out_ref[along(i), :] = dot(turned(block, i * (chunk // height), -1), ah_ref[...]).astype(BF16)

    each(rows // chunk, back)


def whole(count):
    return [pl.BlockSpec(memory_space=VMEM)] * count


def body(facets, sub_offsets, col_offsets, screen_index, screens):
    axes = ("facet", "col")
    facet_now = lax.axis_index("facet")
    facet_count = lax.axis_size("facet")
    column_count = lax.axis_size("col")
    devices = facet_count * column_count
    local_rows, slab = facets.shape[1], facets.shape[3]
    height = local_rows * column_count
    rows = facet_count * height
    subgrid_count = sub_offsets.shape[1]
    owned = subgrid_count // facet_count
    size = screens.shape[2]
    span = -(-(XC + STEP * (facet_count - 1)) // LANES) * LANES
    chunk = max(height, min(rows, CHUNK))
    dims = (facet_count, height, span, slab, size, owned, chunk)

    mine = facets[0].reshape(local_rows, 2 * slab)
    everyone = lax.all_to_all(
        jnp.tile(mine, (devices, 1)), axes, split_axis=0, concat_axis=0, tiled=True
    )
    own_offsets = lax.dynamic_slice(sub_offsets[0], (facet_now * owned,), (owned,))
    table_shapes = [
        ((2 * slab, 2 * span), BF16),
        ((owned, 2 * span, rows), BF16),
        ((size, 2 * span), BF16),
        ((2 * span, 2 * size), BF16),
        ((2 * size, 2 * span), BF16),
        ((2 * span, size), BF16),
        ((owned, rows, 2 * span), BF16),
        ((2 * span, 2 * slab), BF16),
        ((owned, 2, size, size), F32),
    ]
    table_bytes = sum(math.prod(s) * jnp.dtype(t).itemsize for s, t in table_shapes)
    tables = pl.pallas_call(
        functools.partial(tables_kernel, dims),
        out_shape=[jax.ShapeDtypeStruct(s, t) for s, t in table_shapes],
        in_specs=[pl.BlockSpec(memory_space=pltpu.MemorySpace.SMEM)] * 3
        + [pl.BlockSpec(memory_space=pl.ANY)],
        out_specs=whole(len(table_shapes)),
        scratch_shapes=[pltpu.SemaphoreType.DMA((owned,))],
        cost_estimate=pl.CostEstimate(
            flops=100 * table_bytes, bytes_accessed=2 * table_bytes, transcendentals=0
        ),
        name="tables",
    )(col_offsets, own_offsets, screen_index[0], screens)
    terms = pl.pallas_call(
        functools.partial(main_kernel, dims),
        out_shape=jax.ShapeDtypeStruct((rows, 2 * slab), BF16),
        in_specs=whole(1 + len(tables)),
        out_specs=pl.BlockSpec(memory_space=VMEM),
        scratch_shapes=[pltpu.VMEM((rows, 2 * span), BF16)],
        name="window",
    )(everyone, *tables)
    arrived = lax.all_to_all(terms, axes, split_axis=0, concat_axis=0, tiled=True)
    factor = 1.0 / math.sqrt(column_count * subgrid_count)
    summed = jnp.sum(arrived.reshape(devices, local_rows, 2 * slab).astype(F32), axis=0) * factor
    return summed.reshape(1, local_rows, 2, slab)


def solution(mesh):
    return jax.shard_map(
        body,
        mesh=mesh,
        in_specs=(P("facet", "col", None, None), P("col", None), P("col"), P("col", "facet"), P()),
        out_specs=P("facet", "col", None, None),
        check_vma=False,
    )
```

time: 103 us -> 33.1 us (0.32)
  waiting for transfers between devices: 31.7 us -> 3.34 us
  matrix products: 25.2 us -> 0 us
  between operations: 15.1 us -> 1.34 us
  blocking collectives: 18.4 us -> 10.8 us
  Pallas kernels: 0 us -> 6.7 us
  other arithmetic: 4.49 us -> 0.04 us
  starting transfers between devices: 4.87 us -> 7.33 us
    reduce_scatter x1 -> x0, waiting for transfers between devices: 29.2 us -> none  [body(): lax.psum_scatter(jnp.stack([summand[0], summand[1]], axis=1), 'col', scat...]
    dot_general x28 -> x0, matrix products: 24.3 us -> none  [the longest x12 15.4 us: single(): jnp.einsum(form, left_part, right_part, preferred_element_type=jnp.float32)]
    all_gather x1 -> x0, blocking collectives: 10.3 us -> none  [body(): whole_slab = lax.all_gather(facets[0], 'col', axis=0, tiled=True)]
    pallas_call x0 -> x2, Pallas kernels: none -> 6.7 us  [the longest x1 3.75 us: body(): pl.pallas_call(functools.partial(main_kernel, dims), out_shape=jax.ShapeD...]
    all_to_all x1, blocking collectives: 8.11 us -> 10.8 us  [body(): lax.all_to_all(terms, axes, split_axis=0, concat_axis=0, tiled=True)]
    all_to_all x1, starting transfers between devices: 4.87 us -> 7.33 us  [body(): lax.all_to_all(jnp.tile(mine, (devices, 1)), axes, split_axis=0, concat_a...]
    neg x1 -> x0, other arithmetic: 1.07 us -> none  [body(): adjoint_embed = (embedding[0], -embedding[1])]
    convert_element_type x1 -> x0, other arithmetic: 1.07 us -> none  [phase_pair(): (jnp.cos(angles) * factor).astype(jnp.bfloat16)]
  transfers between devices with their start and end apart: 2 -> 1, of which waited for: 2 -> 1; matrix products, arithmetic and copies ran while one was open for 2% -> 2% of each run, Pallas kernels for 0% -> 9%
where the time goes in v1:
time: 33.1 us; the launch traced here: 32.7 us
  blocking collectives  10.8 us (33%)
  starting transfers between devices  7.33 us (22%)
  Pallas kernels  6.7 us (20%)
  waiting for transfers between devices  3.34 us (10%)
  local copies, waits for them, and re-layouts  3.22 us (10%)
  between operations  1.34 us (4%)
    all_to_all x1, blocking collectives, body(): lax.all_to_all(terms, axes, split_axis=0, concat_axis=0, tiled=True)  10.8 us
    all_to_all x1, starting transfers between devices, body(): lax.all_to_all(jnp.tile(mine, (devices, 1)), axes, split_axis=0, concat_a...  7.33 us
    pallas_call x1, Pallas kernels, body(): pl.pallas_call(functools.partial(main_kernel, dims), out_shape=jax.ShapeD...  3.75 us
    all_to_all x1, waiting for transfers between devices, body(): lax.all_to_all(jnp.tile(mine, (devices, 1)), axes, split_axis=0, concat_a...  3.34 us
    pallas_call x1, Pallas kernels, body(): pl.pallas_call(functools.partial(tables_kernel, dims), out_shape=[jax.Sha...  2.96 us
    unnamed x5, local copies, waits for them, and re-layouts  1.36 us
    another operation x1, local copies, waits for them, and re-layouts, body(): jnp.tile(mine, (devices, 1))  0.66 us
  transfers between devices with their start and end apart: 1, of which 1 were waited for; matrix products, arithmetic and copies ran while one was open for 2% of the time, Pallas kernels for 9%

profile of v1, /device:TPU:0, one launch (start us, length us, event | category | flops | bytes accessed | tf_op | source)
XLA Modules:
  0.0 32.7 jit_solution(674647997215012834)
XLA Ops:
  0.0 0.0 copy-start
  0.0 0.7 %copy.8 = bf16[1,8,2,128]{3,1,2,0:T(8,128)(2,1)S(1)} copy(bf16[1,8,2,128]{3,2,1,0:T(2,128)(2,1)} %param.5) | data formatting | bytes 8192
  0.7 0.7 %tile.9 = bf16[32,8,256]{2,1,0:T(8,128)(2,1)} broadcast(bf16[8,256]{1,0:T(8,128)(2,1)S(1)} %bitcast.12), dimensions={1,2} | broadcast | bytes 135168 | tf_op jit(solution)/shard_map/tile | solution.py:223
  1.4 7.3 %all-to-all-start = ((bf16[32,8,256]{2,1,0:T(8,128)(2,1)}), bf16[32,8,256]{2,1,0:T(8,128)(2,1)S(1)}, u32[]{:S(2)}, u32[]{:S(2)}) async-start(bf16[32,8,256]{2,1,0:T(8,128)(2,1)} %tile.9), calls=%async_computation | async-start | bytes 262144 | tf_op jit(solution)/shard_map/all_to_all | solution.py:222
  10.0 0.0 copy-done
  10.0 0.6 %constant_dynamic-slice_fusion = s32[1,1]{1,0:T(1,128)} fusion(s32[1,4]{1,0:T(1,128)S(1)} %copy-done, s32[]{:T(128)S(6)} %select_n.3), kind=kLoop, calls=%fused_computation.3 | loop fusion | bytes 12 | tf_op jit(solution)/shard_map/dynamic_slice | solution.py:225
  10.6 3.0 %tables.1 = (bf16[256,256]{1,0:T(8,128)(2,1)}, bf16[1,256,256]{2,1,0:T(8,128)(2,1)}, bf16[256,256]{1,0:T(8,128)(2,1)}, bf16[256,512]{1,0:T(8,128)(2,1)}, bf16[51...) custom-call(s32[1]{0:T(128)S(6)} %copy.9.col_ref, ...), custom_call_target="tpu_custom_call" | custom-call | flops 183500800 | bytes 3670016 | tf_op jit(solution)/shard_map/tables/pallas_call | solution.py:238
  13.6 3.3 %all-to-all-done = bf16[32,8,256]{2,1,0:T(8,128)(2,1)S(1)} async-done(((bf16[32,8,256]{2,1,0:T(8,128)(2,1)}), bf16[32,8,256]{2,1,0:T(8,128)(2,1)S(1)}, u32[]{:S(2)}, u32[]{:S(2)}) %all-to-all-start) | async-done | bytes 131104 | tf_op jit(solution)/shard_map/all_to_all | solution.py:222
  16.9 0.0 copy-start.1
  16.9 0.7 %copy-done.1 = bf16[32,8,256]{2,1,0:T(8,128)(2,1)} copy-done((bf16[32,8,256]{2,1,0:T(8,128)(2,1)}, bf16[32,8,256]{2,1,0:T(8,128)(2,1)S(1)}, u32[]{:S(2)}) %copy-start.1) | copy-done | bytes 131096
  17.6 3.7 %window.1 = bf16[256,256]{1,0:T(8,128)(2,1)} custom-call(bf16[256,256]{1,0:T(8,128)(2,1)} %bitcast.10, bf16[256,256]{1,0:T(8,128)(2,1)} %get-tuple-element.14.a_ref, bf16[1,256,256]{2,1,0:T(8,128)(2,1)} %get-tuple-element.15.p_ref, bf16[256,256]{1,0:T(8,128)(2,1)} %get-tuple-element.16.w_ref, bf16[256,512]{1,0:T(8,128)(2,1)} %get-tuple-element.17.wt_ref, ...), custom_call_target="tpu_custom_call" | custom-call | tf_op jit(solution)/shard_map/window/pallas_call | solution.py:250
  21.3 10.8 %all_to_all.17 = bf16[32,8,256]{2,1,0:T(8,128)(2,1)S(1)} all-to-all(bf16[32,8,256]{2,1,0:T(8,128)(2,1)} %bitcast.11), channel_id=1, replica_groups=mesh['facet'=4,'col'=8] {'facet','col'}, dimensions={0} | all-to-all | bytes 262144 | tf_op jit(solution)/shard_map/all_to_all | solution.py:258
  32.1 0.6 %mul.18 = f32[1,8,2,128]{3,2,1,0:T(2,128)} reshape(f32[8,256]{1,0:T(8,128)S(1)} %broadcast_multiply_fusion) | data formatting | bytes 16384 | tf_op jit(solution)/shard_map/mul | solution.py:260
  (2 shorter events, 0.0 us)
Async XLA Ops:
  0.0 10.0 %copy-start = (s32[1,4]{1,0:T(1,128)S(1)}, s32[1,4]{1,0:T(1,128)}, u32[]{:S(2)}) copy-start(s32[1,4]{1,0:T(1,128)} %param.6) | copy-start | bytes 52
  1.4 15.5 %all-to-all-start = ((bf16[32,8,256]{2,1,0:T(8,128)(2,1)}), bf16[32,8,256]{2,1,0:T(8,128)(2,1)S(1)}, u32[]{:S(2)}, u32[]{:S(2)}) async-start(bf16[32,8,256]{2,1,0:T(8,128)(2,1)} %tile.9), calls=%async_computation | async-start | bytes 262144 | tf_op jit(solution)/shard_map/all_to_all | solution.py:222
  16.9 0.7 %copy-start.1 = (bf16[32,8,256]{2,1,0:T(8,128)(2,1)}, bf16[32,8,256]{2,1,0:T(8,128)(2,1)S(1)}, u32[]{:S(2)}) copy-start(bf16[32,8,256]{2,1,0:T(8,128)(2,1)S(1)} %all-to-all-done) | copy-start | bytes 393220

commit v2 on v1

--- a/solution.py
+++ b/solution.py
@@ -13,6 +13,7 @@
 STEP = 7
 LANES = 128
 CHUNK = 256
+VMEM_LIMIT = 24 * 2**20
 F32 = jnp.float32
 BF16 = jnp.bfloat16
 VMEM = pltpu.MemorySpace.VMEM
@@ -46,63 +47,14 @@
 
 
 def tables_kernel(
-    dims, col_ref, sub_ref, pick_ref, screens_ref,
-    a_ref, p_ref, w_ref, wt_ref, wc_ref, wh_ref, ph_ref, ah_ref, gain_ref, sem,
+    dims, numbers_hbm, screens_ref,
+    a_ref, p_ref, w_ref, wt_ref, wc_ref, wh_ref, ph_ref, ah_ref, gain_ref,
+    numbers_ref, small_sem, sem,
 ):
     facets, height, span, slab, size, owned, chunk = dims
     rows = facets * height
-    copies = [
-        pltpu.make_async_copy(screens_ref.at[pick_ref[k]], gain_ref.at[k], sem.at[k])
-        for k in range(owned)
-    ]
-    for copy in copies:
-        copy.start()
-    shift = height.bit_length() - 1
-
-    def phases(p, row, offset):
-        u = p - STEP * (row >> shift)
-        frequency = (offset + u) & (NPAD - 1)
-        number = (frequency * (row & (NPAD - 1))) & (NPAD - 1)
-        inside = (u >= 0) & (u < XC)
-        real, imag = wave(number, NPAD, 1.0 / math.sqrt(height))
-        zero = jnp.zeros_like(real)
-        return jnp.where(inside, real, zero).astype(BF16), jnp.where(inside, -imag, zero).astype(BF16)
-
-    def row_chunk(k, i):
-        base = i * chunk
-        along = pl.ds(pl.multiple_of(base, chunk), chunk) if not isinstance(i, int) else pl.ds(base, chunk)
-        shape = (span, chunk)
-        real, imag = phases(iota(shape, 0), iota(shape, 1) + base, sub_ref[k])
-        p_ref[k, :span, along] = real
-        p_ref[k, span:, along] = imag
-        shape = (chunk, span)
-        real, imag = phases(iota(shape, 1), iota(shape, 0) + base, sub_ref[k])
-        ph_ref[k, along, :span] = real
-        ph_ref[k, along, span:] = imag
-
-    for k in range(owned):
-        each(rows // chunk, functools.partial(row_chunk, k))
-
-    def across(x, v):
-        frequency = (col_ref[0] + v) & (NPAD - 1)
-        number = (x * frequency) & (NPAD - 1)
-        real, imag = wave(number, NPAD, 1.0 / math.sqrt(slab))
-        zero = jnp.zeros_like(real)
-        inside = v < XC
-        return jnp.where(inside, real, zero).astype(BF16), jnp.where(inside, -imag, zero).astype(BF16)
-
-    shape = (slab, span)
-    real, imag = across(iota(shape, 0), iota(shape, 1))
-    a_ref[:slab, :span] = real
-    a_ref[:slab, span:] = imag
-    a_ref[slab:, :span] = -imag
-    a_ref[slab:, span:] = real
-    shape = (span, slab)
-    real, imag = across(iota(shape, 1), iota(shape, 0))
-    ah_ref[:span, :slab] = real
-    ah_ref[:span, slab:] = -imag
-    ah_ref[span:, :slab] = imag
-    ah_ref[span:, slab:] = real
+    small = pltpu.make_async_copy(numbers_hbm, numbers_ref, small_sem)
+    small.start()
 
     scale = 1.0 / math.sqrt(size)
     shape = (size, span)
@@ -124,6 +76,62 @@
     wt_ref[:span, size:] = imag
     wt_ref[span:, :size] = -imag
     wt_ref[span:, size:] = real
+
+    small.wait()
+    copies = [
+        pltpu.make_async_copy(screens_ref.at[numbers_ref[1 + k]], gain_ref.at[k], sem.at[k])
+        for k in range(owned)
+    ]
+    for copy in copies:
+        copy.start()
+    first = 1 + owned + lax.axis_index("facet") * owned
+    shift = height.bit_length() - 1
+
+    def phases(p, row, offset):
+        u = p - STEP * (row >> shift)
+        frequency = (offset + u) & (NPAD - 1)
+        number = (frequency * (row & (NPAD - 1))) & (NPAD - 1)
+        inside = (u >= 0) & (u < XC)
+        real, imag = wave(number, NPAD, 1.0 / math.sqrt(height))
+        zero = jnp.zeros_like(real)
+        return jnp.where(inside, real, zero).astype(BF16), jnp.where(inside, -imag, zero).astype(BF16)
+
+    def row_chunk(k, i):
+        base = i * chunk
+        along = pl.ds(pl.multiple_of(base, chunk), chunk) if not isinstance(i, int) else pl.ds(base, chunk)
+        shape = (span, chunk)
+        real, imag = phases(iota(shape, 0), iota(shape, 1) + base, numbers_ref[first + k])
+        p_ref[k, :span, along] = real
+        p_ref[k, span:, along] = imag
+        shape = (chunk, span)
+        real, imag = phases(iota(shape, 1), iota(shape, 0) + base, numbers_ref[first + k])
+        ph_ref[k, along, :span] = real
+        ph_ref[k, along, span:] = imag
+
+    for k in range(owned):
+        each(rows // chunk, functools.partial(row_chunk, k))
+
+    def across(x, v):
+        frequency = (numbers_ref[0] + v) & (NPAD - 1)
+        number = (x * frequency) & (NPAD - 1)
+        real, imag = wave(number, NPAD, 1.0 / math.sqrt(slab))
+        zero = jnp.zeros_like(real)
+        inside = v < XC
+        return jnp.where(inside, real, zero).astype(BF16), jnp.where(inside, -imag, zero).astype(BF16)
+
+    shape = (slab, span)
+    real, imag = across(iota(shape, 0), iota(shape, 1))
+    a_ref[:slab, :span] = real
+    a_ref[:slab, span:] = imag
+    a_ref[slab:, :span] = -imag
+    a_ref[slab:, span:] = real
+    shape = (span, slab)
+    real, imag = across(iota(shape, 1), iota(shape, 0))
+    ah_ref[:span, :slab] = real
+    ah_ref[:span, slab:] = -imag
+    ah_ref[span:, :slab] = imag
+    ah_ref[span:, slab:] = real
+
     for copy in copies:
         copy.wait()
 
@@ -198,13 +206,24 @@
     each(rows // chunk, back)
 
 
+def send_kernel(facets_ref, out_ref, mine_ref, sem):
+    copy = pltpu.make_async_copy(facets_ref, mine_ref, sem)
+    copy.start()
+    copy.wait()
+    mine = jnp.concatenate([mine_ref[0, :, 0, :], mine_ref[0, :, 1, :]], axis=1)
+    out_ref[...] = jnp.broadcast_to(mine[None], out_ref.shape)
+
+
+def in_hbm(array):
+    return pltpu.with_memory_space_constraint(array, pltpu.MemorySpace.HBM)
+
+
 def whole(count):
     return [pl.BlockSpec(memory_space=VMEM)] * count
 
 
 def body(facets, sub_offsets, col_offsets, screen_index, screens):
     axes = ("facet", "col")
-    facet_now = lax.axis_index("facet")
     facet_count = lax.axis_size("facet")
     column_count = lax.axis_size("col")
     devices = facet_count * column_count
@@ -218,11 +237,18 @@
     chunk = max(height, min(rows, CHUNK))
     dims = (facet_count, height, span, slab, size, owned, chunk)
 
-    mine = facets[0].reshape(local_rows, 2 * slab)
-    everyone = lax.all_to_all(
-        jnp.tile(mine, (devices, 1)), axes, split_axis=0, concat_axis=0, tiled=True
-    )
-    own_offsets = lax.dynamic_slice(sub_offsets[0], (facet_now * owned,), (owned,))
+    outgoing = pl.pallas_call(
+        send_kernel,
+        out_shape=jax.ShapeDtypeStruct((devices, local_rows, 2 * slab), BF16),
+        in_specs=[pl.BlockSpec(memory_space=pl.ANY)],
+        out_specs=pl.BlockSpec(memory_space=VMEM),
+        scratch_shapes=[pltpu.VMEM(facets.shape, BF16), pltpu.SemaphoreType.DMA],
+        compiler_params=pltpu.CompilerParams(vmem_limit_bytes=VMEM_LIMIT),
+        name="send",
+    )(in_hbm(facets))
+    everyone = lax.all_to_all(outgoing, axes, split_axis=0, concat_axis=0, tiled=True)
+    everyone = everyone.reshape(rows, 2 * slab)
+    numbers = jnp.concatenate([col_offsets, screen_index[0], sub_offsets[0]])
     table_shapes = [
         ((2 * slab, 2 * span), BF16),
         ((owned, 2 * span, rows), BF16),
@@ -238,26 +264,32 @@
     tables = pl.pallas_call(
         functools.partial(tables_kernel, dims),
         out_shape=[jax.ShapeDtypeStruct(s, t) for s, t in table_shapes],
-        in_specs=[pl.BlockSpec(memory_space=pltpu.MemorySpace.SMEM)] * 3
-        + [pl.BlockSpec(memory_space=pl.ANY)],
+        in_specs=[pl.BlockSpec(memory_space=pl.ANY)] * 2,
         out_specs=whole(len(table_shapes)),
-        scratch_shapes=[pltpu.SemaphoreType.DMA((owned,))],
+        scratch_shapes=[
+            pltpu.SMEM(numbers.shape, jnp.int32),
+            pltpu.SemaphoreType.DMA,
+            pltpu.SemaphoreType.DMA((owned,)),
+        ],
+        compiler_params=pltpu.CompilerParams(vmem_limit_bytes=VMEM_LIMIT),
         cost_estimate=pl.CostEstimate(
             flops=100 * table_bytes, bytes_accessed=2 * table_bytes, transcendentals=0
         ),
         name="tables",
-    )(col_offsets, own_offsets, screen_index[0], screens)
+    )(numbers, in_hbm(screens))
     terms = pl.pallas_call(
         functools.partial(main_kernel, dims),
         out_shape=jax.ShapeDtypeStruct((rows, 2 * slab), BF16),
         in_specs=whole(1 + len(tables)),
         out_specs=pl.BlockSpec(memory_space=VMEM),
         scratch_shapes=[pltpu.VMEM((rows, 2 * span), BF16)],
+        compiler_params=pltpu.CompilerParams(vmem_limit_bytes=VMEM_LIMIT),
         name="window",
     )(everyone, *tables)
+    terms = terms.reshape(devices, local_rows, 2 * slab)
     arrived = lax.all_to_all(terms, axes, split_axis=0, concat_axis=0, tiled=True)
     factor = 1.0 / math.sqrt(column_count * subgrid_count)
-    summed = jnp.sum(arrived.reshape(devices, local_rows, 2 * slab).astype(F32), axis=0) * factor
+    summed = jnp.sum(arrived.astype(F32), axis=0) * factor
     return summed.reshape(1, local_rows, 2, slab)
 
 

time: 33.1 us -> 29.4 us (0.89)
  local copies, waits for them, and re-layouts: 3.22 us -> 0.61 us
  Pallas kernels: 6.7 us -> 4.54 us
  waiting for transfers between devices: 3.34 us -> 4.57 us
  blocking collectives: 10.8 us -> 9.97 us
  other arithmetic: 0.04 us -> 0.77 us
    pallas_call x1, Pallas kernels: 3.75 us -> 1.56 us  [body(): pl.pallas_call(functools.partial(main_kernel, dims), out_shape=jax.ShapeD...]
    pallas_call x0 -> x1, Pallas kernels: none -> 1.37 us  [body(): pl.pallas_call(send_kernel, out_shape=jax.ShapeDtypeStruct((devices, loca...]
    unnamed x5 -> x0, local copies, waits for them, and re-layouts: 1.36 us -> none
    pallas_call x1, Pallas kernels: 2.96 us -> 1.6 us  [body(): pl.pallas_call(functools.partial(tables_kernel, dims), out_shape=[jax.Sha...]
    all_to_all x1, waiting for transfers between devices: 3.34 us -> 4.57 us  [body(): lax.all_to_all(outgoing, axes, split_axis=0, concat_axis=0, tiled=True)]
    all_to_all x1, blocking collectives: 10.8 us -> 9.97 us  [body(): lax.all_to_all(terms, axes, split_axis=0, concat_axis=0, tiled=True)]
    concatenate x0 -> x1, other arithmetic: none -> 0.73 us  [body(): numbers = jnp.concatenate([col_offsets, screen_index[0], sub_offsets[0]])]
    another operation x1 -> x0, local copies, waits for them, and re-layouts: 0.66 us -> none  [body(): jnp.tile(mine, (devices, 1))]
  transfers between devices with their start and end apart: 1 -> 1, of which waited for: 1 -> 1; matrix products, arithmetic and copies ran while one was open for 2% -> 3% of each run, Pallas kernels for 9% -> 6%
where the time goes in v2:
time: 29.4 us; the launch traced here: 29.1 us
  blocking collectives  9.97 us (34%)
  starting transfers between devices  7.33 us (25%)
  waiting for transfers between devices  4.57 us (16%)
  Pallas kernels  4.54 us (15%)
  between operations  1.34 us (5%)
  other arithmetic  0.77 us (3%)
  local copies, waits for them, and re-layouts  0.61 us (2%)
    all_to_all x1, blocking collectives, body(): lax.all_to_all(terms, axes, split_axis=0, concat_axis=0, tiled=True)  9.97 us
    all_to_all x1, starting transfers between devices, body(): lax.all_to_all(outgoing, axes, split_axis=0, concat_axis=0, tiled=True)  7.33 us
    all_to_all x1, waiting for transfers between devices, body(): lax.all_to_all(outgoing, axes, split_axis=0, concat_axis=0, tiled=True)  4.57 us
    pallas_call x1, Pallas kernels, body(): pl.pallas_call(functools.partial(tables_kernel, dims), out_shape=[jax.Sha...  1.6 us
    pallas_call x1, Pallas kernels, body(): pl.pallas_call(functools.partial(main_kernel, dims), out_shape=jax.ShapeD...  1.56 us
    pallas_call x1, Pallas kernels, body(): pl.pallas_call(send_kernel, out_shape=jax.ShapeDtypeStruct((devices, loca...  1.37 us
    concatenate x1, other arithmetic, body(): numbers = jnp.concatenate([col_offsets, screen_index[0], sub_offsets[0]])  0.73 us
    mul x1, local copies, waits for them, and re-layouts, body(): summed = jnp.sum(arrived.astype(F32), axis=0) * factor  0.61 us
  transfers between devices with their start and end apart: 1, of which 1 were waited for; matrix products, arithmetic and copies ran while one was open for 3% of the time, Pallas kernels for 6%

profile of v2, /device:TPU:0, one launch (start us, length us, event | category | flops | bytes accessed | tf_op | source)
XLA Modules:
  0.0 29.1 jit_solution(16113071242939752047)
XLA Ops:
  0.0 1.4 %send.1 = bf16[32,8,256]{2,1,0:T(8,128)(2,1)} custom-call(bf16[1,8,2,128]{3,2,1,0:T(2,128)(2,1)} %facets_ref.1), custom_call_target="tpu_custom_call" | custom-call | tf_op jit(solution)/shard_map/send/pallas_call | solution.py:240
  1.4 7.3 %all-to-all-start = ((bf16[32,8,256]{2,1,0:T(8,128)(2,1)}), bf16[32,8,256]{2,1,0:T(8,128)(2,1)S(1)}, u32[]{:S(2)}, u32[]{:S(2)}) async-start(bf16[32,8,256]{2,1,0:T(8,128)(2,1)} %send.1), calls=%async_computation | async-start | bytes 262144 | tf_op jit(solution)/shard_map/all_to_all | solution.py:249
  10.0 0.7 %pad_add_fusion.numbers_hbm = s32[6]{0:T(128)S(1)} fusion(s32[4]{0:T(128)} %bitcast.7, s32[1]{0:T(128)} %bitcast.4, s32[1]{0:T(128)S(6)} %copy.6), kind=kLoop, calls=%fused_computation.2 | loop fusion | flops 12 | bytes 48 | tf_op jit(solution)/shard_map/concatenate | solution.py:251
  10.7 1.6 %tables.1 = (bf16[256,256]{1,0:T(8,128)(2,1)S(1)}, bf16[1,256,256]{2,1,0:T(8,128)(2,1)S(1)}, bf16[256,256]{1,0:T(8,128)(2,1)S(1)}, bf16[256,512]{1,0:T(8,128)(2,...) custom-call(s32[6]{0:T(128)S(1)} %pad_add_fusion.numbers_hbm, ...), custom_call_target="tpu_custom_call" | custom-call | flops 183500800 | bytes 3670016 | tf_op jit(solution)/shard_map/tables/pallas_call | solution.py:264
  12.4 4.6 %all-to-all-done = bf16[32,8,256]{2,1,0:T(8,128)(2,1)S(1)} async-done(((bf16[32,8,256]{2,1,0:T(8,128)(2,1)}), bf16[32,8,256]{2,1,0:T(8,128)(2,1)S(1)}, u32[]{:S(2)}, u32[]{:S(2)}) %all-to-all-start) | async-done | bytes 131104 | tf_op jit(solution)/shard_map/all_to_all | solution.py:249
  16.9 1.6 %window.1 = bf16[256,256]{1,0:T(8,128)(2,1)S(1)} custom-call(bf16[256,256]{1,0:T(8,128)(2,1)S(1)} %bitcast.5, bf16[256,256]{1,0:T(8,128)(2,1)S(1)} %get-tuple-element.14.a_ref, bf16[1,256,256]{2,1,0:T(8,128)(2,1)S(1)} %get-tuple-element.15.p_ref, bf16[256,256]{1,0:T(8,128)(2,1)S(1)} %get-tuple-element.16.w_ref, ...), custom_call_target="tpu_custom_call" | custom-call | tf_op jit(solution)/shard_map/window/pallas_call | solution.py:280
  18.5 10.0 %all_to_all.10 = bf16[32,8,256]{2,1,0:T(8,128)(2,1)S(1)} all-to-all(bf16[32,8,256]{2,1,0:T(8,128)(2,1)S(1)} %bitcast.6), channel_id=1, replica_groups=mesh['facet'=4,'col'=8] {'facet','col'}, dimensions={0} | all-to-all | bytes 262144 | tf_op jit(solution)/shard_map/all_to_all | solution.py:290
  28.5 0.6 %mul.18 = f32[1,8,2,128]{3,2,1,0:T(2,128)} reshape(f32[8,256]{1,0:T(8,128)S(1)} %broadcast_multiply_fusion) | data formatting | bytes 16384 | tf_op jit(solution)/shard_map/mul | solution.py:292
  (2 shorter events, 0.0 us)
Async XLA Ops:
  1.4 15.5 %all-to-all-start = ((bf16[32,8,256]{2,1,0:T(8,128)(2,1)}), bf16[32,8,256]{2,1,0:T(8,128)(2,1)S(1)}, u32[]{:S(2)}, u32[]{:S(2)}) async-start(bf16[32,8,256]{2,1,0:T(8,128)(2,1)} %send.1), calls=%async_computation | async-start | bytes 262144 | tf_op jit(solution)/shard_map/all_to_all | solution.py:249

commit v3 on v2

v3 whole, which is shorter than its diff:
```python
import functools
import math

import jax
import jax.numpy as jnp
from jax import lax
from jax.experimental import pallas as pl
from jax.experimental.pallas import tpu as pltpu
from jax.sharding import PartitionSpec as P

XC = 64
NPAD = 8192
STEP = 7
ROWS = 8
LANES = 128
CHUNK = 256
VMEM_LIMIT = 24 * 2**20
F32 = jnp.float32
BF16 = jnp.bfloat16
VMEM = pltpu.MemorySpace.VMEM


def wave(number, period, scale):
    quarter = period // 4
    bits = quarter.bit_length() - 1
    turn = (number + quarter // 2) >> bits
    angle = (number - (turn << bits)).astype(F32) * (2.0 * math.pi / period)
    square = angle * angle
    sine = angle * (1.0 + square * (-1 / 6 + square * (1 / 120 + square * (-1 / 5040))))
    cosine = 1.0 + square * (-1 / 2 + square * (1 / 24 + square * (-1 / 720 + square * (1 / 40320))))
    odd = (turn & 1) == 1
    first = jnp.where(odd, sine, cosine)
    second = jnp.where(odd, cosine, sine)
    first = jnp.where(((turn + 1) & 2) == 2, -scale, scale) * first
    second = jnp.where((turn & 2) == 2, -scale, scale) * second
    return first, second


def each(count, step):
    if count == 1:
        step(0)
    else:
        lax.fori_loop(0, count, lambda i, c: (step(i), c)[1], 0)


def iota(shape, axis):
    return lax.broadcasted_iota(jnp.int32, shape, axis)


def ladder(first, step, count):
    real, imag = first
    reals, imags = [real], [imag]
    for _ in range(count - 1):
        real, imag = real * step[0] - imag * step[1], real * step[1] + imag * step[0]
        reals.append(real)
        imags.append(imag)
    return jnp.concatenate(reals, axis=0), jnp.concatenate(imags, axis=0)


def fourier(rows, row_start, lane_numbers, period, scale):
    shape = (ROWS, lane_numbers.shape[1])
    lanes = jnp.broadcast_to(lane_numbers, shape) & (period - 1)
    top = (iota(shape, 0) + row_start) & (period - 1)
    first = wave((top * lanes) & (period - 1), period, scale)
    return ladder(first, wave((ROWS * lanes) & (period - 1), period, 1.0), rows // ROWS)


def block(real, imag, flip):
    low, high = (imag, -imag) if flip else (-imag, imag)
    return jnp.concatenate(
        [jnp.concatenate([real, high], axis=1), jnp.concatenate([low, real], axis=1)], axis=0
    )


def tables_kernel(
    dims, numbers_hbm, screens_ref,
    a_ref, wp_ref, wt_ref, w_ref, wph_ref, ah_ref, gain_ref,
    numbers_ref, small_sem, sem,
):
    facets, height, span, slab, size, owned, chunk = dims
    rows = facets * height
    small = pltpu.make_async_copy(numbers_hbm, numbers_ref, small_sem)
    small.start()

    scale = 1.0 / math.sqrt(size)
    real, imag = fourier(size, 0, iota((1, span), 1), size, scale)
    w_real, w_imag = real.astype(BF16), imag.astype(BF16)
    w_both = jnp.concatenate([w_real, w_imag], axis=1)
    w_ref[...] = w_both
    real, imag = fourier(span, 0, iota((1, size), 1), size, scale)
    wt_ref[...] = block(real.astype(BF16), imag.astype(BF16), False)

    small.wait()
    copies = [
        pltpu.make_async_copy(screens_ref.at[numbers_ref[1 + k]], gain_ref.at[k], sem.at[k])
        for k in range(owned)
    ]
    for copy in copies:
        copy.start()
    column = numbers_ref[0]

    def facet_tables(f):
        lag = STEP * f
        lanes = iota((1, span), 1) - lag
        scale = 1.0 / math.sqrt(slab)
        real, imag = fourier(slab, 0, column + lanes, NPAD, scale / math.sqrt(facets))
        inside = jnp.broadcast_to((lanes >= 0) & (lanes < XC), real.shape)
        zero = jnp.zeros_like(real)
        a_ref[f] = block(
            jnp.where(inside, real, zero).astype(BF16),
            jnp.where(inside, -imag, zero).astype(BF16),
            False,
        )
        real, imag = fourier(span, column - lag, iota((1, slab), 1), NPAD, scale)
        down = iota(real.shape, 0) - lag
        inside = (down >= 0) & (down < XC)
        zero = jnp.zeros_like(real)
        ah_ref[f] = block(
            jnp.where(inside, real, zero).astype(BF16),
            jnp.where(inside, -imag, zero).astype(BF16),
            True,
        )

    if rows == chunk:
        for f in range(facets):
            facet_tables(f)
    else:
        each(facets, facet_tables)

    first = 1 + owned + lax.axis_index("facet") * owned
    scale = 1.0 / math.sqrt(height)
    shift = height.bit_length() - 1

    def row_chunk(k, i):
        fixed = isinstance(i, int)
        base = i * chunk

        def along(start):
            return pl.ds(start, chunk) if fixed else pl.ds(pl.multiple_of(start, chunk), chunk)

        offset = numbers_ref[first + k]
        row = iota((1, chunk), 1) + base
        lag = STEP * (row >> shift)
        low = jnp.broadcast_to((offset - lag) & (NPAD - 1), (ROWS, chunk))
        lanes = jnp.broadcast_to(row & (NPAD - 1), (ROWS, chunk))
        top = (low + iota((ROWS, chunk), 0)) & (NPAD - 1)
        real, imag = ladder(
            wave((top * lanes) & (NPAD - 1), NPAD, scale),
            wave((ROWS * lanes) & (NPAD - 1), NPAD, 1.0),
            span // ROWS,
        )
        u = iota((span, chunk), 0) - lag
        inside = (u >= 0) & (u < XC)
        zero = jnp.zeros_like(real)
        real = jnp.where(inside, real, zero).astype(BF16)
        imag = jnp.where(inside, -imag, zero).astype(BF16)
        both = dot(w_both, block(real, imag, False)).astype(BF16)
        wp_ref[k, :size, along(base)] = both[:, :chunk]
        wp_ref[k, size:, along(base)] = both[:, chunk:]
        reals, imags = [], []
        for f in range(chunk // height):
            lag = STEP * ((base >> shift) + f)
            lanes = iota((1, span), 1) - lag
            real, imag = fourier(height, base + f * height, lanes + offset, NPAD, scale)
            inside = jnp.broadcast_to((lanes >= 0) & (lanes < XC), real.shape)
            zero = jnp.zeros_like(real)
            reals.append(jnp.where(inside, real, zero).astype(BF16))
            imags.append(jnp.where(inside, -imag, zero).astype(BF16))
        both = jnp.concatenate(
            [jnp.concatenate(reals, axis=0), jnp.concatenate(imags, axis=0)], axis=1
        )
        wph_ref[k, along(base), :] = dot(both, wt_ref[...]).astype(BF16)

    for k in range(owned):
        each(rows // chunk, functools.partial(row_chunk, k))
    for copy in copies:
        copy.wait()


def dot(first, second):
    return jnp.dot(first, second, preferred_element_type=F32)


def main_kernel(
    dims, x_ref, a_ref, wp_ref, wt_ref, w_ref, wph_ref, ah_ref, gain_ref, out_ref, spread_ref,
):
    facets, height, span, slab, size, owned, chunk = dims
    rows = facets * height

    def by_facet(value, i, table_ref):
        parts = []
        for f in range(chunk // height):
            own = value[f * height : (f + 1) * height]
            parts.append(dot(own, table_ref[i * (chunk // height) + f]).astype(BF16))
        return parts[0] if len(parts) == 1 else jnp.concatenate(parts, axis=0)

    def along(i):
        base = i * chunk
        return pl.ds(base, chunk) if isinstance(i, int) else pl.ds(pl.multiple_of(base, chunk), chunk)

    def spread(i):
        spread_ref[along(i), :] = by_facet(x_ref[along(i), :], i, a_ref)

    each(rows // chunk, spread)
    inners = []
    for k in range(owned):
        first = dot(wp_ref[k, :size], spread_ref[...])
        second = dot(wp_ref[k, size:], spread_ref[...])
        half = jnp.concatenate(
            [first[:, :span] - second[:, span:], first[:, span:] + second[:, :span]], axis=1
        ).astype(BF16)
        grid = dot(half, wt_ref[...])
        real, imag = grid[:, :size], grid[:, size:]
        gain_real, gain_imag = gain_ref[k, 0], gain_ref[k, 1]
        seen_real = (real * gain_real - imag * gain_imag).astype(BF16)
        seen_imag = (real * gain_imag + imag * gain_real).astype(BF16)
        first = dot(seen_real, w_ref[...])
        second = dot(seen_imag, w_ref[...])
        inners.append(
            jnp.concatenate(
                [first[:, :span] + second[:, span:], second[:, :span] - first[:, span:]], axis=1
            ).astype(BF16)
        )

    def back(i):
        own = 0.0
        for k in range(owned):
            first = dot(wph_ref[k, along(i), :size], inners[k])
            second = dot(wph_ref[k, along(i), size:], inners[k])
            own += jnp.concatenate(
                [first[:, :span] + second[:, span:], first[:, span:] - second[:, :span]], axis=1
            )
        out_ref[along(i), :] = by_facet(own.astype(BF16), i, ah_ref)

    each(rows // chunk, back)


def send_kernel(facets_ref, out_ref, mine_ref, sem):
    copy = pltpu.make_async_copy(facets_ref, mine_ref, sem)
    copy.start()
    copy.wait()
    mine = jnp.concatenate([mine_ref[0, :, 0, :], mine_ref[0, :, 1, :]], axis=1)
    out_ref[...] = jnp.broadcast_to(mine[None], out_ref.shape)


def in_hbm(array):
    return pltpu.with_memory_space_constraint(array, pltpu.MemorySpace.HBM)


def whole(count):
    return [pl.BlockSpec(memory_space=VMEM)] * count


def body(facets, sub_offsets, col_offsets, screen_index, screens):
    axes = ("facet", "col")
    facet_count = lax.axis_size("facet")
    column_count = lax.axis_size("col")
    devices = facet_count * column_count
    local_rows, slab = facets.shape[1], facets.shape[3]
    height = local_rows * column_count
    rows = facet_count * height
    subgrid_count = sub_offsets.shape[1]
    owned = subgrid_count // facet_count
    size = screens.shape[2]
    span = -(-(XC + STEP * (facet_count - 1)) // LANES) * LANES
    chunk = max(height, min(rows, CHUNK))
    dims = (facet_count, height, span, slab, size, owned, chunk)

    outgoing = pl.pallas_call(
        send_kernel,
        out_shape=jax.ShapeDtypeStruct((devices, local_rows, 2 * slab), BF16),
        in_specs=[pl.BlockSpec(memory_space=pl.ANY)],
        out_specs=pl.BlockSpec(memory_space=VMEM),
        scratch_shapes=[pltpu.VMEM(facets.shape, BF16), pltpu.SemaphoreType.DMA],
        compiler_params=pltpu.CompilerParams(vmem_limit_bytes=VMEM_LIMIT),
        name="send",
    )(in_hbm(facets))
    everyone = lax.all_to_all(outgoing, axes, split_axis=0, concat_axis=0, tiled=True)
    everyone = everyone.reshape(rows, 2 * slab)
    numbers = jnp.concatenate([col_offsets, screen_index[0], sub_offsets[0]])
    table_shapes = [
        ((facet_count, 2 * slab, 2 * span), BF16),
        ((owned, 2 * size, rows), BF16),
        ((2 * span, 2 * size), BF16),
        ((size, 2 * span), BF16),
        ((owned, rows, 2 * size), BF16),
        ((facet_count, 2 * span, 2 * slab), BF16),
        ((owned, 2, size, size), F32),
    ]
    table_bytes = sum(math.prod(s) * jnp.dtype(t).itemsize for s, t in table_shapes)
    tables = pl.pallas_call(
        functools.partial(tables_kernel, dims),
        out_shape=[jax.ShapeDtypeStruct(s, t) for s, t in table_shapes],
        in_specs=[pl.BlockSpec(memory_space=pl.ANY)] * 2,
        out_specs=whole(len(table_shapes)),
        scratch_shapes=[
            pltpu.SMEM(numbers.shape, jnp.int32),
            pltpu.SemaphoreType.DMA,
            pltpu.SemaphoreType.DMA((owned,)),
        ],
        compiler_params=pltpu.CompilerParams(vmem_limit_bytes=VMEM_LIMIT),
        cost_estimate=pl.CostEstimate(
            flops=100 * table_bytes, bytes_accessed=2 * table_bytes, transcendentals=0
        ),
        name="tables",
    )(numbers, in_hbm(screens))
    terms = pl.pallas_call(
        functools.partial(main_kernel, dims),
        out_shape=jax.ShapeDtypeStruct((rows, 2 * slab), BF16),
        in_specs=whole(1 + len(tables)),
        out_specs=pl.BlockSpec(memory_space=VMEM),
        scratch_shapes=[pltpu.VMEM((rows, 2 * span), BF16)],
        compiler_params=pltpu.CompilerParams(vmem_limit_bytes=VMEM_LIMIT),
        name="window",
    )(everyone, *tables)
    terms = terms.reshape(devices, local_rows, 2 * slab)
    arrived = lax.all_to_all(terms, axes, split_axis=0, concat_axis=0, tiled=True)
    factor = 1.0 / math.sqrt(column_count * subgrid_count)
    summed = jnp.sum(arrived.astype(F32), axis=0) * factor
    return summed.reshape(1, local_rows, 2, slab)


def solution(mesh):
    return jax.shard_map(
        body,
        mesh=mesh,
        in_specs=(P("facet", "col", None, None), P("col", None), P("col"), P("col", "facet"), P()),
        out_specs=P("facet", "col", None, None),
        check_vma=False,
    )
```

time: 29.4 us -> 28.8 us (0.980)
  Pallas kernels: 4.54 us -> 3.97 us
    pallas_call x1, Pallas kernels: 1.56 us -> 0.99 us  [body(): pl.pallas_call(functools.partial(main_kernel, dims), out_shape=jax.ShapeD...]
where the time goes in v3:
time: 28.8 us; the launch traced here: 28.6 us
  blocking collectives  9.97 us (35%)
  starting transfers between devices  7.33 us (25%)
  waiting for transfers between devices  4.56 us (16%)
  Pallas kernels  3.97 us (14%)
  between operations  1.34 us (5%)
  other arithmetic  0.77 us (3%)
  local copies, waits for them, and re-layouts  0.61 us (2%)
    all_to_all x1, blocking collectives, body(): lax.all_to_all(terms, axes, split_axis=0, concat_axis=0, tiled=True)  9.97 us
    all_to_all x1, starting transfers between devices, body(): lax.all_to_all(outgoing, axes, split_axis=0, concat_axis=0, tiled=True)  7.33 us
    all_to_all x1, waiting for transfers between devices, body(): lax.all_to_all(outgoing, axes, split_axis=0, concat_axis=0, tiled=True)  4.56 us
    pallas_call x1, Pallas kernels, body(): pl.pallas_call(functools.partial(tables_kernel, dims), out_shape=[jax.Sha...  1.61 us
    pallas_call x1, Pallas kernels, body(): pl.pallas_call(send_kernel, out_shape=jax.ShapeDtypeStruct((devices, loca...  1.37 us
    pallas_call x1, Pallas kernels, body(): pl.pallas_call(functools.partial(main_kernel, dims), out_shape=jax.ShapeD...  0.99 us
    concatenate x1, other arithmetic, body(): numbers = jnp.concatenate([col_offsets, screen_index[0], sub_offsets[0]])  0.73 us
    mul x1, local copies, waits for them, and re-layouts, body(): summed = jnp.sum(arrived.astype(F32), axis=0) * factor  0.61 us
  transfers between devices with their start and end apart: 1, of which 1 were waited for; matrix products, arithmetic and copies ran while one was open for 3% of the time, Pallas kernels for 6%

profile of v3, /device:TPU:0, one launch (start us, length us, event | category | flops | bytes accessed | tf_op | source)
XLA Modules:
  0.0 28.6 jit_solution(12650265612851502600)
XLA Ops:
  0.0 1.4 %send.1 = bf16[32,8,256]{2,1,0:T(8,128)(2,1)} custom-call(bf16[1,8,2,128]{3,2,1,0:T(2,128)(2,1)} %facets_ref.1), custom_call_target="tpu_custom_call" | custom-call | tf_op jit(solution)/shard_map/send/pallas_call | solution.py:269
  1.4 7.3 %all-to-all-start = ((bf16[32,8,256]{2,1,0:T(8,128)(2,1)}), bf16[32,8,256]{2,1,0:T(8,128)(2,1)S(1)}, u32[]{:S(2)}, u32[]{:S(2)}) async-start(bf16[32,8,256]{2,1,0:T(8,128)(2,1)} %send.1), calls=%async_computation | async-start | bytes 262144 | tf_op jit(solution)/shard_map/all_to_all | solution.py:278
  10.0 0.7 %pad_add_fusion.numbers_hbm = s32[6]{0:T(128)S(1)} fusion(s32[4]{0:T(128)} %bitcast.7, s32[1]{0:T(128)} %bitcast.4, s32[1]{0:T(128)S(6)} %copy.6), kind=kLoop, calls=%fused_computation.2 | loop fusion | flops 12 | bytes 48 | tf_op jit(solution)/shard_map/concatenate | solution.py:280
  10.7 1.6 %tables.1 = (bf16[4,256,256]{2,1,0:T(8,128)(2,1)S(1)}, bf16[1,512,256]{2,1,0:T(8,128)(2,1)S(1)}, bf16[256,512]{1,0:T(8,128)(2,1)S(1)}, bf16[256,256]{1,0:T(8,128...) custom-call(s32[6]{0:T(128)S(1)} %pad_add_fusion.numbers_hbm, ...), custom_call_target="tpu_custom_call" | custom-call | flops 249036800 | bytes 4980736 | tf_op jit(solution)/shard_map/tables/pallas_call | solution.py:291
  12.4 4.6 %all-to-all-done = bf16[32,8,256]{2,1,0:T(8,128)(2,1)S(1)} async-done(((bf16[32,8,256]{2,1,0:T(8,128)(2,1)}), bf16[32,8,256]{2,1,0:T(8,128)(2,1)S(1)}, u32[]{:S(2)}, u32[]{:S(2)}) %all-to-all-start) | async-done | bytes 131104 | tf_op jit(solution)/shard_map/all_to_all | solution.py:278
  16.9 1.0 %window.1 = bf16[256,256]{1,0:T(8,128)(2,1)S(1)} custom-call(bf16[256,256]{1,0:T(8,128)(2,1)S(1)} %bitcast.5, bf16[4,256,256]{2,1,0:T(8,128)(2,1)S(1)} %get-tuple-element.12.a_ref, bf16[1,512,256]{2,1,0:T(8,128)(2,1)S(1)} %get-tuple-element.13.wp_ref, bf16[256,512]{1,0:T(8,128)(2,1)S(1)} %get-tuple-element.14.wt_ref, ...), custom_call_target="tpu_custom_call" | custom-call | tf_op jit(solution)/shard_map/window/pallas_call | solution.py:307
  17.9 10.0 %all_to_all.10 = bf16[32,8,256]{2,1,0:T(8,128)(2,1)S(1)} all-to-all(bf16[32,8,256]{2,1,0:T(8,128)(2,1)S(1)} %bitcast.6), channel_id=1, replica_groups=mesh['facet'=4,'col'=8] {'facet','col'}, dimensions={0} | all-to-all | bytes 262144 | tf_op jit(solution)/shard_map/all_to_all | solution.py:317
  27.9 0.6 %mul.18 = f32[1,8,2,128]{3,2,1,0:T(2,128)} reshape(f32[8,256]{1,0:T(8,128)S(1)} %broadcast_multiply_fusion) | data formatting | bytes 16384 | tf_op jit(solution)/shard_map/mul | solution.py:319
  (2 shorter events, 0.0 us)
Async XLA Ops:
  1.4 15.5 %all-to-all-start = ((bf16[32,8,256]{2,1,0:T(8,128)(2,1)}), bf16[32,8,256]{2,1,0:T(8,128)(2,1)S(1)}, u32[]{:S(2)}, u32[]{:S(2)}) async-start(bf16[32,8,256]{2,1,0:T(8,128)(2,1)} %send.1), calls=%async_computation | async-start | bytes 262144 | tf_op jit(solution)/shard_map/all_to_all | solution.py:278

commit v4 on v3

--- a/solution.py
+++ b/solution.py
@@ -14,6 +14,8 @@
 ROWS = 8
 LANES = 128
 CHUNK = 256
+HALF = 7
+UNROLL = False
 VMEM_LIMIT = 24 * 2**20
 F32 = jnp.float32
 BF16 = jnp.bfloat16
@@ -235,6 +237,280 @@
     each(rows // chunk, back)
 
 
+def pair_send_kernel(facets_ref, sub_hbm, col_ref, pick_ref, out_ref, mine_ref, sub_ref, sem):
+    copies = [
+        pltpu.make_async_copy(facets_ref, mine_ref, sem.at[0]),
+        pltpu.make_async_copy(sub_hbm, sub_ref, sem.at[1]),
+    ]
+    for copy in copies:
+        copy.start()
+    for copy in copies:
+        copy.wait()
+    numbers = (col_ref[0], sub_ref[0, lax.axis_index("facet")], pick_ref[0, 0])
+    lane = iota((facets_ref.shape[1], LANES), 1)
+    told = jnp.zeros(lane.shape, jnp.int32)
+    for i, number in enumerate(numbers):
+        told = jnp.where(lane == i, number >> HALF, told)
+        told = jnp.where(lane == i + len(numbers), number & ((1 << HALF) - 1), told)
+    mine = jnp.concatenate(
+        [mine_ref[0, :, 0, :], mine_ref[0, :, 1, :], told.astype(F32).astype(BF16)], axis=1
+    )
+    out_ref[...] = jnp.broadcast_to(mine[None], out_ref.shape)
+
+
+def fine_dot(first, second):
+    parts = []
+    for value in (first, second):
+        high = value.astype(BF16)
+        parts.append((high, (value - high.astype(F32)).astype(BF16)))
+    (a, a_rest), (b, b_rest) = parts
+    return dot(a, b) + (dot(a, b_rest) + dot(a_rest, b))
+
+
+def pair_tables_kernel(
+    dims, screens_hbm, a_ref, wp_ref, wt_ref, low_ref, wa_ref, screens_ref, sem
+):
+    facets, height, span, slab, size, columns, local = dims
+    rows = facets * height
+    copy = pltpu.make_async_copy(screens_hbm, screens_ref, sem)
+    copy.start()
+    scale = 1.0 / math.sqrt(size)
+    w_both = jnp.concatenate(fourier(size, 0, iota((1, span), 1), size, scale), axis=1)
+    w_turned = block(*fourier(span, 0, iota((1, size), 1), size, scale), False)
+    wt_ref[...] = w_turned.astype(BF16)
+
+    def keep(number, real, imag):
+        inside = jnp.broadcast_to((number >= 0) & (number < XC), real.shape)
+        zero = jnp.zeros_like(real)
+        return jnp.where(inside, real, zero), jnp.where(inside, -imag, zero)
+
+    facet = lax.axis_index("facet")
+    lag = STEP * facet
+    scale = 1.0 / math.sqrt(slab)
+    for f in range(facets):
+        lanes = iota((1, span), 1) - STEP * f
+        real, imag = keep(lanes, *fourier(slab, 0, lanes, NPAD, scale / math.sqrt(facets)))
+        a_ref[f] = block(real.astype(BF16), imag.astype(BF16), False)
+    real, imag = fourier(span, -lag, iota((1, slab), 1), NPAD, scale)
+    both = fine_dot(w_both, block(*keep(iota(real.shape, 0) - lag, real, imag), False))
+    wa_ref[:, :slab] = both[:, :slab].astype(BF16)
+    wa_ref[:, slab:] = (-both[:, slab:]).astype(BF16)
+
+    scale = 1.0 / math.sqrt(height)
+    row = iota((1, rows), 1)
+    behind = STEP * (row >> (height.bit_length() - 1))
+    lanes = jnp.broadcast_to(row & (NPAD - 1), (ROWS, rows))
+    top = (jnp.broadcast_to(-behind, (ROWS, rows)) + iota((ROWS, rows), 0)) & (NPAD - 1)
+    real, imag = ladder(
+        wave((top * lanes) & (NPAD - 1), NPAD, scale),
+        wave((ROWS * lanes) & (NPAD - 1), NPAD, 1.0),
+        span // ROWS,
+    )
+    both = fine_dot(w_both, block(*keep(iota(real.shape, 0) - behind, real, imag), False)).astype(BF16)
+    wp_ref[:size] = both[:, :rows]
+    wp_ref[size:] = both[:, rows:]
+
+    pair_rows = 2 * local
+    base = facet * height + (lax.axis_index("col") >> 1) * pair_rows
+    lanes = iota((1, span), 1) - lag
+    real, imag = keep(lanes, *fourier(pair_rows, base, lanes, NPAD, scale))
+    both = fine_dot(jnp.concatenate([real, imag], axis=1), w_turned).astype(BF16)
+    low_ref[:pair_rows] = both[:, :size]
+    low_ref[pair_rows:] = both[:, size:]
+    copy.wait()
+
+
+def dot_nt(first, second):
+    return lax.dot_general(first, second, (((1,), (1,)), ((), ())), preferred_element_type=F32)
+
+
+def pair_kernel(
+    dims, x_ref, a_ref, wp_ref, wt_ref, low_ref, wa_ref, screens_ref, mine_ref, other_ref,
+    told_ref, numbers_ref, spread_ref, down_ref, half_ref, lifted_ref, seen_ref, gathered_ref, phase_ref, sem,
+):
+    facets, height, span, slab, size, columns, local = dims
+    rows = facets * height
+    subgrids = facets
+    pair_rows = 2 * local
+    mine_columns = columns // 2
+    core = lax.axis_index("col") & 1
+    base = lax.axis_index("facet") * height + (lax.axis_index("col") >> 1) * pair_rows
+
+    lane, line = iota((ROWS, LANES), 1), iota((ROWS, LANES), 0)
+    weights = jnp.where(lane == line, 1 << HALF, jnp.where(lane == line + 3, 1, 0))
+    weights = jnp.where(line < 3, weights, 0).astype(F32).astype(BF16)
+    told = dot_nt(weights, x_ref[:, 2 * slab :])
+    told_ref[...] = told.astype(jnp.int32)
+    copy = pltpu.make_async_copy(told_ref, numbers_ref, sem)
+    copy.start()
+    copy.wait()
+
+    def number(kind, facet, column):
+        return numbers_ref[kind, (facet * columns + column) * local]
+
+    def times(a, b):
+        return a[0] * b[0] - a[1] * b[1], a[0] * b[1] + a[1] * b[0]
+
+    def phases(offset, where):
+        real, imag = wave((where * offset) & (NPAD - 1), NPAD, 1.0)
+        return real, -imag
+
+    for i in range(mine_columns):
+        column = 2 * i + core
+        ahead = phases(number(0, 0, column), iota((ROWS, slab), 1))
+        phase_ref[2 * i * ROWS : (2 * i + 1) * ROWS, :] = ahead[0]
+        phase_ref[(2 * i + 1) * ROWS : (2 * i + 2) * ROWS, :] = ahead[1]
+        line = iota((ROWS, rows), 0)
+        offset_rows = jnp.zeros((ROWS, rows), jnp.int32)
+        for s in range(subgrids):
+            offset_rows = jnp.where(line == s, number(1, s, column), offset_rows)
+        row_phase = phases(offset_rows, iota((ROWS, rows), 1))
+        for h in (0, 1):
+            down_ref[i, h, :, :ROWS] = row_phase[h].T
+        own = x_ref[:, : 2 * slab].astype(F32)
+        real, imag = times(
+            (own[:, :slab], own[:, slab:]),
+            [jnp.broadcast_to(p[:1], (rows, slab)) for p in ahead],
+        )
+        turned = jnp.concatenate([real.astype(BF16), imag.astype(BF16)], axis=1)
+        for f in range(facets):
+            part = slice(f * height, (f + 1) * height)
+            spread_ref[i, part, :] = dot(turned[part], a_ref[f])
+
+    def one_column(i):
+        for s in range(subgrids):
+            down = [jnp.broadcast_to(down_ref[i, h, :, s : s + 1], (rows, span)) for h in (0, 1)]
+            real, imag = times((spread_ref[i, :, :span], spread_ref[i, :, span:]), down)
+            lifted_ref[s, :, :span] = real.astype(BF16)
+            lifted_ref[s, :, span:] = imag.astype(BF16)
+        for s in range(subgrids):
+            lifted = lifted_ref[s]
+            first = dot(wp_ref[:size], lifted)
+            second = dot(wp_ref[size:], lifted)
+            half_ref[s * size : (s + 1) * size, :span] = (first[:, :span] - second[:, span:]).astype(BF16)
+            half_ref[s * size : (s + 1) * size, span:] = (first[:, span:] + second[:, :span]).astype(BF16)
+        half = half_ref[...]
+        all_real, all_imag = dot(half, wt_ref[:, :size]), dot(half, wt_ref[:, size:])
+        for s in range(subgrids):
+            part = slice(s * size, (s + 1) * size)
+            real, imag = all_real[part], all_imag[part]
+            pick = number(2, s, 2 * i + core)
+            gain_real, gain_imag = screens_ref[pick, 0], screens_ref[pick, 1]
+            seen_ref[s, 0] = (real * gain_real - imag * gain_imag).astype(BF16)
+            seen_ref[s, 1] = (real * gain_imag + imag * gain_real).astype(BF16)
+        sums = None
+        for s in range(subgrids):
+            first = dot(low_ref[...], seen_ref[s, 0])
+            second = dot(low_ref[...], seen_ref[s, 1])
+            real = first[:pair_rows] + second[pair_rows:]
+            imag = second[:pair_rows] - first[pair_rows:]
+            back = [
+                jnp.broadcast_to(down_ref[i, h, pl.ds(base, pair_rows), s : s + 1], (pair_rows, size))
+                for h in (0, 1)
+            ]
+            term = times((real, imag), (back[0], -back[1]))
+            sums = term if sums is None else (sums[0] + term[0], sums[1] + term[1])
+        start = pl.multiple_of(i * pair_rows, pair_rows)
+        gathered_ref[pl.ds(start, pair_rows), :size] = sums[0].astype(BF16)
+        gathered_ref[pl.ds(start, pair_rows), size:] = sums[1].astype(BF16)
+
+    lax.fori_loop(0, mine_columns, lambda i, c: (one_column(i), c)[1], 0)
+
+    first = dot(gathered_ref[:, :size], wa_ref[...])
+    second = dot(gathered_ref[:, size:], wa_ref[...])
+    real = first[:, :slab] - second[:, slab:]
+    imag = first[:, slab:] + second[:, :slab]
+    total = None
+    for i in range(mine_columns):
+        part = slice(i * pair_rows, (i + 1) * pair_rows)
+        back_real = jnp.broadcast_to(phase_ref[i * 2 * ROWS : i * 2 * ROWS + 1], (pair_rows, slab))
+        back_imag = jnp.broadcast_to(
+            phase_ref[i * 2 * ROWS + ROWS : i * 2 * ROWS + ROWS + 1], (pair_rows, slab)
+        )
+        term = times((real[part], imag[part]), (back_real, -back_imag))
+        total = term if total is None else (total[0] + term[0], total[1] + term[1])
+    both = jnp.concatenate(total, axis=1)
+    mine_ref[...] = jnp.where(core == 0, both[:local], both[local:])
+    other_ref[...] = jnp.where(core == 0, both[local:], both[:local])
+
+
+def pair_body(facets, sub_offsets, col_offsets, screen_index, screens):
+    facet_count = lax.axis_size("facet")
+    column_count = lax.axis_size("col")
+    devices = facet_count * column_count
+    local_rows, slab = facets.shape[1], facets.shape[3]
+    height = local_rows * column_count
+    rows = facet_count * height
+    subgrid_count = sub_offsets.shape[1]
+    size = screens.shape[2]
+    span = -(-(XC + STEP * (facet_count - 1)) // LANES) * LANES
+    dims = (facet_count, height, span, slab, size, column_count, local_rows)
+    any_space = pl.BlockSpec(memory_space=pl.ANY)
+    smem = pl.BlockSpec(memory_space=pltpu.MemorySpace.SMEM)
+    width = 2 * slab + LANES
+
+    outgoing = pl.pallas_call(
+        pair_send_kernel,
+        out_shape=jax.ShapeDtypeStruct((devices, local_rows, width), BF16),
+        in_specs=[any_space, any_space, smem, smem],
+        out_specs=pl.BlockSpec(memory_space=VMEM),
+        scratch_shapes=[
+            pltpu.VMEM(facets.shape, BF16),
+            pltpu.SMEM(sub_offsets.shape, jnp.int32),
+            pltpu.SemaphoreType.DMA((2,)),
+        ],
+        compiler_params=pltpu.CompilerParams(vmem_limit_bytes=VMEM_LIMIT),
+        name="send",
+    )(in_hbm(facets), in_hbm(sub_offsets), col_offsets, screen_index)
+    everyone = lax.all_to_all(
+        outgoing, ("facet", "col"), split_axis=0, concat_axis=0, tiled=True
+    ).reshape(rows, width)
+    table_shapes = [
+        ((facet_count, 2 * span, 2 * slab), BF16),
+        ((2 * size, rows), BF16),
+        ((2 * span, 2 * size), BF16),
+        ((4 * local_rows, size), BF16),
+        ((size, 2 * slab), BF16),
+        (screens.shape, F32),
+    ]
+    table_bytes = sum(math.prod(s) * jnp.dtype(t).itemsize for s, t in table_shapes)
+    tables = pl.pallas_call(
+        functools.partial(pair_tables_kernel, dims),
+        out_shape=[jax.ShapeDtypeStruct(s, t) for s, t in table_shapes],
+        in_specs=[any_space],
+        out_specs=whole(len(table_shapes)),
+        scratch_shapes=[pltpu.SemaphoreType.DMA],
+        compiler_params=pltpu.CompilerParams(vmem_limit_bytes=VMEM_LIMIT),
+        cost_estimate=pl.CostEstimate(
+            flops=100 * table_bytes, bytes_accessed=2 * table_bytes, transcendentals=0
+        ),
+        name="tables",
+    )(in_hbm(screens))
+    mine, other = pl.pallas_call(
+        functools.partial(pair_kernel, dims),
+        out_shape=[jax.ShapeDtypeStruct((local_rows, 2 * slab), F32)] * 2,
+        in_specs=whole(1 + len(tables)),
+        out_specs=whole(2),
+        scratch_shapes=[
+            pltpu.VMEM((ROWS, rows), jnp.int32),
+            pltpu.SMEM((ROWS, rows), jnp.int32),
+            pltpu.VMEM((column_count // 2, rows, 2 * span), F32),
+            pltpu.VMEM((column_count // 2, 2, rows, LANES), F32),
+            pltpu.VMEM((subgrid_count * size, 2 * span), BF16),
+            pltpu.VMEM((subgrid_count, rows, 2 * span), BF16),
+            pltpu.VMEM((subgrid_count, 2, size, size), BF16),
+            pltpu.VMEM((column_count * local_rows, 2 * size), BF16),
+            pltpu.VMEM((column_count * ROWS, slab), F32),
+            pltpu.SemaphoreType.DMA,
+        ],
+        compiler_params=pltpu.CompilerParams(vmem_limit_bytes=VMEM_LIMIT),
+        name="window",
+    )(everyone, *tables)
+    swap = [(i, i ^ 1) for i in range(column_count)]
+    summed = mine + lax.ppermute(other, "col", swap)
+    return (summed / math.sqrt(column_count * subgrid_count)).reshape(1, local_rows, 2, slab)
+
+
 def send_kernel(facets_ref, out_ref, mine_ref, sem):
     copy = pltpu.make_async_copy(facets_ref, mine_ref, sem)
     copy.start()
@@ -251,7 +527,7 @@
     return [pl.BlockSpec(memory_space=VMEM)] * count
 
 
-def body(facets, sub_offsets, col_offsets, screen_index, screens):
+def spread_body(facets, sub_offsets, col_offsets, screen_index, screens):
     axes = ("facet", "col")
     facet_count = lax.axis_size("facet")
     column_count = lax.axis_size("col")
@@ -320,6 +596,13 @@
     return summed.reshape(1, local_rows, 2, slab)
 
 
+def body(facets, sub_offsets, col_offsets, screen_index, screens):
+    columns, subgrids = lax.axis_size("col"), sub_offsets.shape[1]
+    alone = columns % 2 == 0 and subgrids == lax.axis_size("facet") and columns * subgrids <= 32
+    run = pair_body if alone else spread_body
+    return run(facets, sub_offsets, col_offsets, screen_index, screens)
+
+
 def solution(mesh):
     return jax.shard_map(
         body,

time: 28.8 us -> 27.3 us (0.948)
  blocking collectives: 9.97 us -> 0 us
  Pallas kernels: 3.97 us -> 9.07 us
  waiting for transfers between devices: 4.56 us -> 8.16 us
  other arithmetic: 0.77 us -> 0.01 us
  starting transfers between devices: 7.33 us -> 7.9 us
    all_to_all x1 -> x0, blocking collectives: 9.97 us -> none  [body(): lax.all_to_all(terms, axes, split_axis=0, concat_axis=0, tiled=True)]
    pallas_call x3, Pallas kernels: 3.97 us -> 9.07 us  [the longest x1 5.94 us: pair_body(): pl.pallas_call(functools.partial(pair_kernel, dims), out_shape=[jax.Shape...]
    all_to_all x1, waiting for transfers between devices: 4.56 us -> 7.33 us  [pair_body(): lax.all_to_all(outgoing, ('facet', 'col'), split_axis=0, concat_axis=0, t...]
    ppermute x0 -> x1, waiting for transfers between devices: none -> 0.83 us  [pair_body(): summed = mine + lax.ppermute(other, 'col', swap)]
    concatenate x1 -> x0, other arithmetic: 0.73 us -> none  [body(): numbers = jnp.concatenate([col_offsets, screen_index[0], sub_offsets[0]])]
    mul x1 -> x0, local copies, waits for them, and re-layouts: 0.61 us -> none  [body(): summed = jnp.sum(arrived.astype(F32), axis=0) * factor]
    reshape x0 -> x1, local copies, waits for them, and re-layouts: none -> 0.61 us  [pair_body(): (summed / math.sqrt(column_count * subgrid_count)).reshape(1, local_rows,...]
    ppermute x0 -> x1, starting transfers between devices: none -> 0.57 us  [pair_body(): summed = mine + lax.ppermute(other, 'col', swap)]
  transfers between devices with their start and end apart: 1 -> 2, of which waited for: 1 -> 2; matrix products, arithmetic and copies ran while one was open for 3% -> 0% of each run, Pallas kernels for 6% -> 6%
where the time goes in v4:
time: 27.3 us; the launch traced here: 27.1 us
  Pallas kernels  9.07 us (33%)
  waiting for transfers between devices  8.16 us (30%)
  starting transfers between devices  7.9 us (29%)
  between operations  1.33 us (5%)
  local copies, waits for them, and re-layouts  0.61 us (2%)
    all_to_all x1, starting transfers between devices, pair_body(): lax.all_to_all(outgoing, ('facet', 'col'), split_axis=0, concat_axis=0, t...  7.33 us
    all_to_all x1, waiting for transfers between devices, pair_body(): lax.all_to_all(outgoing, ('facet', 'col'), split_axis=0, concat_axis=0, t...  7.33 us
    pallas_call x1, Pallas kernels, pair_body(): pl.pallas_call(functools.partial(pair_kernel, dims), out_shape=[jax.Shape...  5.94 us
    pallas_call x1, Pallas kernels, pair_body(): pl.pallas_call(functools.partial(pair_tables_kernel, dims), out_shape=[ja...  1.61 us
    pallas_call x1, Pallas kernels, pair_body(): pl.pallas_call(pair_send_kernel, out_shape=jax.ShapeDtypeStruct((devices,...  1.52 us
    ppermute x1, waiting for transfers between devices, pair_body(): summed = mine + lax.ppermute(other, 'col', swap)  0.83 us
    reshape x1, local copies, waits for them, and re-layouts, pair_body(): (summed / math.sqrt(column_count * subgrid_count)).reshape(1, local_rows,...  0.61 us
    ppermute x1, starting transfers between devices, pair_body(): summed = mine + lax.ppermute(other, 'col', swap)  0.57 us
  transfers between devices with their start and end apart: 2, of which 2 were waited for; matrix products, arithmetic and copies ran while one was open for 0% of the time, Pallas kernels for 6%

profile of v4, /device:TPU:0, one launch (start us, length us, event | category | flops | bytes accessed | tf_op | source)
XLA Modules:
  0.0 27.1 jit_solution(792211545130321460)
XLA Ops:
  1.3 1.5 %send.1 = bf16[32,8,384]{2,1,0:T(8,128)(2,1)} custom-call(bf16[1,8,2,128]{3,2,1,0:T(2,128)(2,1)} %facets_ref.1, s32[1,4]{1,0:T(1,128)} %sub_hbm.1, s32[1]{0:T(128)S(6)} %copy.7.col_ref, s32[1,1]{1,0:T(1,128)S(6)} %copy.8.pick_ref), custom_call_target="tpu_custom_call" | custom-call | tf_op jit(solution)/shard_map/send/pallas_call | solution.py:452
  2.8 7.3 %all-to-all-start = ((bf16[32,8,384]{2,1,0:T(8,128)(2,1)}), bf16[32,8,384]{2,1,0:T(8,128)(2,1)S(1)}, u32[]{:S(2)}, u32[]{:S(2)}) async-start(bf16[32,8,384]{2,1,0:T(8,128)(2,1)} %send.1), calls=%async_computation | async-start | bytes 393216 | tf_op jit(solution)/shard_map/all_to_all | solution.py:465
  10.2 1.6 %tables.1 = (bf16[4,256,256]{2,1,0:T(8,128)(2,1)S(1)}, bf16[512,256]{1,0:T(8,128)(2,1)S(1)}, bf16[256,512]{1,0:T(8,128)(2,1)S(1)}, bf16[32,256]{1,0:T(8,128)(2,1...) custom-call(f32[4,2,256,256]{3,2,1,0:T(8,128)} %screens_hbm.1), custom_call_target="tpu_custom_call" | custom-call | flops 329318400 | bytes 6586368 | tf_op jit(solution)/shard_map/tables/pallas_call | solution.py:477
  11.8 7.3 %all-to-all-done = bf16[32,8,384]{2,1,0:T(8,128)(2,1)S(1)} async-done(((bf16[32,8,384]{2,1,0:T(8,128)(2,1)}), bf16[32,8,384]{2,1,0:T(8,128)(2,1)S(1)}, u32[]{:S(2)}, u32[]{:S(2)}) %all-to-all-start) | async-done | bytes 196640 | tf_op jit(solution)/shard_map/all_to_all | solution.py:465
  19.1 5.9 %window.1 = (f32[8,256]{1,0:T(8,128)S(1)}, f32[8,256]{1,0:T(8,128)S(1)}) custom-call(bf16[256,384]{1,0:T(8,128)(2,1)S(1)} %bitcast.3, bf16[4,256,256]{2,1,0:T(8,128)(2,1)S(1)} %get-tuple-element.13.a_ref, bf16[512,256]{1,0:T(8,128)(2,1)S(1)} %get-tuple-element.14.wp_ref, bf16[256,512]{1,0:T(8,128)(2,1)S(1)} %get-tuple-element.15.wt_ref, ...), custom_call_target="tpu_custom_call" | custom-call | tf_op jit(solution)/shard_map/window/pallas_call | solution.py:489
  25.1 0.6 %collective-permute-start = (f32[8,256]{1,0:T(8,128)S(1)}, f32[8,256]{1,0:T(8,128)S(1)}, u32[]{:S(2)}, u32[]{:S(2)}) collective-permute-start(f32[8,256]{1,0:T(8,128)S(1)} %get-tuple-element.20), channel_id=1, source_target_pairs={{0,1},{1,0},{2,3},{3,2},{4,5},{5,4},{6,7},{7,6},{8,9},{9,8},{10,11... | collective-permute-start | bytes 24584 | tf_op jit(solution)/shard_map/ppermute | solution.py:510
  25.6 0.8 %collective-permute-done = f32[8,256]{1,0:T(8,128)S(1)} collective-permute-done((f32[8,256]{1,0:T(8,128)S(1)}, f32[8,256]{1,0:T(8,128)S(1)}, u32[]{:S(2)}, u32[]{:S(2)}) %collective-permute-start) | collective-permute-done | bytes 8224 | tf_op jit(solution)/shard_map/ppermute | solution.py:510
  26.5 0.6 %copy.6 = f32[1,8,2,128]{3,2,1,0:T(2,128)} copy(f32[1,8,2,128]{3,1,2,0:T(8,128)S(1)} %multiply_bitcast_fusion) | data formatting | bytes 16384 | tf_op jit(solution)/shard_map/reshape | solution.py:511
  (1 shorter events, 0.0 us)
Async XLA Ops:
  2.8 16.3 %all-to-all-start = ((bf16[32,8,384]{2,1,0:T(8,128)(2,1)}), bf16[32,8,384]{2,1,0:T(8,128)(2,1)S(1)}, u32[]{:S(2)}, u32[]{:S(2)}) async-start(bf16[32,8,384]{2,1,0:T(8,128)(2,1)} %send.1), calls=%async_computation | async-start | bytes 393216 | tf_op jit(solution)/shard_map/all_to_all | solution.py:465
  25.1 1.4 %collective-permute-start = (f32[8,256]{1,0:T(8,128)S(1)}, f32[8,256]{1,0:T(8,128)S(1)}, u32[]{:S(2)}, u32[]{:S(2)}) collective-permute-start(f32[8,256]{1,0:T(8,128)S(1)} %get-tuple-element.20), channel_id=1, source_target_pairs={{0,1},{1,0},{2,3},{3,2},{4,5},{5,4},{6,7},{7,6},{8,9},{9,8},{10,11... | collective-permute-start | bytes 24584 | tf_op jit(solution)/shard_map/ppermute | solution.py:510

commit v5 on v4

--- a/solution.py
+++ b/solution.py
@@ -377,31 +377,36 @@
             part = slice(f * height, (f + 1) * height)
             spread_ref[i, part, :] = dot(turned[part], a_ref[f])
 
-    def one_column(i):
+    def lift(i, slot):
         for s in range(subgrids):
             down = [jnp.broadcast_to(down_ref[i, h, :, s : s + 1], (rows, span)) for h in (0, 1)]
             real, imag = times((spread_ref[i, :, :span], spread_ref[i, :, span:]), down)
-            lifted_ref[s, :, :span] = real.astype(BF16)
-            lifted_ref[s, :, span:] = imag.astype(BF16)
+            lifted_ref[slot, s, :, :span] = real.astype(BF16)
+            lifted_ref[slot, s, :, span:] = imag.astype(BF16)
+
+    def one_column(i, slot, following):
         for s in range(subgrids):
-            lifted = lifted_ref[s]
+            lifted = lifted_ref[slot, s]
             first = dot(wp_ref[:size], lifted)
             second = dot(wp_ref[size:], lifted)
-            half_ref[s * size : (s + 1) * size, :span] = (first[:, :span] - second[:, span:]).astype(BF16)
-            half_ref[s * size : (s + 1) * size, span:] = (first[:, span:] + second[:, :span]).astype(BF16)
-        half = half_ref[...]
+            part = slice(s * size, (s + 1) * size)
+            half_ref[slot, part, :span] = (first[:, :span] - second[:, span:]).astype(BF16)
+            half_ref[slot, part, span:] = (first[:, span:] + second[:, :span]).astype(BF16)
+        if following is not None:
+            lift(following, 1 - slot)
+        half = half_ref[slot]
         all_real, all_imag = dot(half, wt_ref[:, :size]), dot(half, wt_ref[:, size:])
         for s in range(subgrids):
             part = slice(s * size, (s + 1) * size)
             real, imag = all_real[part], all_imag[part]
             pick = number(2, s, 2 * i + core)
             gain_real, gain_imag = screens_ref[pick, 0], screens_ref[pick, 1]
-            seen_ref[s, 0] = (real * gain_real - imag * gain_imag).astype(BF16)
-            seen_ref[s, 1] = (real * gain_imag + imag * gain_real).astype(BF16)
+            seen_ref[slot, s, 0] = (real * gain_real - imag * gain_imag).astype(BF16)
+            seen_ref[slot, s, 1] = (real * gain_imag + imag * gain_real).astype(BF16)
         sums = None
         for s in range(subgrids):
-            first = dot(low_ref[...], seen_ref[s, 0])
-            second = dot(low_ref[...], seen_ref[s, 1])
+            first = dot(low_ref[...], seen_ref[slot, s, 0])
+            second = dot(low_ref[...], seen_ref[slot, s, 1])
             real = first[:pair_rows] + second[pair_rows:]
             imag = second[:pair_rows] - first[pair_rows:]
             back = [
@@ -410,11 +415,15 @@
             ]
             term = times((real, imag), (back[0], -back[1]))
             sums = term if sums is None else (sums[0] + term[0], sums[1] + term[1])
-        start = pl.multiple_of(i * pair_rows, pair_rows)
-        gathered_ref[pl.ds(start, pair_rows), :size] = sums[0].astype(BF16)
-        gathered_ref[pl.ds(start, pair_rows), size:] = sums[1].astype(BF16)
-
-    lax.fori_loop(0, mine_columns, lambda i, c: (one_column(i), c)[1], 0)
+        part = slice(i * pair_rows, (i + 1) * pair_rows) if isinstance(i, int) else pl.ds(
+            pl.multiple_of(i * pair_rows, pair_rows), pair_rows
+        )
+        gathered_ref[part, :size] = sums[0].astype(BF16)
+        gathered_ref[part, size:] = sums[1].astype(BF16)
+
+    lift(0, 0)
+    for i in range(mine_columns):
+        one_column(i, i % 2, i + 1 if i + 1 < mine_columns else None)
 
     first = dot(gathered_ref[:, :size], wa_ref[...])
     second = dot(gathered_ref[:, size:], wa_ref[...])
@@ -496,9 +505,9 @@
             pltpu.SMEM((ROWS, rows), jnp.int32),
             pltpu.VMEM((column_count // 2, rows, 2 * span), F32),
             pltpu.VMEM((column_count // 2, 2, rows, LANES), F32),
-            pltpu.VMEM((subgrid_count * size, 2 * span), BF16),
-            pltpu.VMEM((subgrid_count, rows, 2 * span), BF16),
-            pltpu.VMEM((subgrid_count, 2, size, size), BF16),
+            pltpu.VMEM((2, subgrid_count * size, 2 * span), BF16),
+            pltpu.VMEM((2, subgrid_count, rows, 2 * span), BF16),
+            pltpu.VMEM((2, subgrid_count, 2, size, size), BF16),
             pltpu.VMEM((column_count * local_rows, 2 * size), BF16),
             pltpu.VMEM((column_count * ROWS, slab), F32),
             pltpu.SemaphoreType.DMA,

time: 27.3 us -> 26.6 us (0.974)
  Pallas kernels: 9.07 us -> 8.3 us
    pallas_call x1, Pallas kernels: 5.94 us -> 5.17 us  [pair_body(): pl.pallas_call(functools.partial(pair_kernel, dims), out_shape=[jax.Shape...]
where the time goes in v5:
time: 26.6 us; the launch traced here: 26.3 us
  Pallas kernels  8.3 us (31%)
  waiting for transfers between devices  8.16 us (31%)
  starting transfers between devices  7.89 us (30%)
  between operations  1.33 us (5%)
  local copies, waits for them, and re-layouts  0.61 us (2%)
    all_to_all x1, starting transfers between devices, pair_body(): lax.all_to_all(outgoing, ('facet', 'col'), split_axis=0, concat_axis=0, t...  7.33 us
    all_to_all x1, waiting for transfers between devices, pair_body(): lax.all_to_all(outgoing, ('facet', 'col'), split_axis=0, concat_axis=0, t...  7.33 us
    pallas_call x1, Pallas kernels, pair_body(): pl.pallas_call(functools.partial(pair_kernel, dims), out_shape=[jax.Shape...  5.17 us
    pallas_call x1, Pallas kernels, pair_body(): pl.pallas_call(functools.partial(pair_tables_kernel, dims), out_shape=[ja...  1.61 us
    pallas_call x1, Pallas kernels, pair_body(): pl.pallas_call(pair_send_kernel, out_shape=jax.ShapeDtypeStruct((devices,...  1.52 us
    ppermute x1, waiting for transfers between devices, pair_body(): summed = mine + lax.ppermute(other, 'col', swap)  0.83 us
    reshape x1, local copies, waits for them, and re-layouts, pair_body(): (summed / math.sqrt(column_count * subgrid_count)).reshape(1, local_rows,...  0.61 us
    ppermute x1, starting transfers between devices, pair_body(): summed = mine + lax.ppermute(other, 'col', swap)  0.56 us
  transfers between devices with their start and end apart: 2, of which 2 were waited for; matrix products, arithmetic and copies ran while one was open for 0% of the time, Pallas kernels for 6%

profile of v5, /device:TPU:0, one launch (start us, length us, event | category | flops | bytes accessed | tf_op | source)
XLA Modules:
  0.0 26.3 jit_solution(13950077805826429209)
XLA Ops:
  1.3 1.5 %send.1 = bf16[32,8,384]{2,1,0:T(8,128)(2,1)} custom-call(bf16[1,8,2,128]{3,2,1,0:T(2,128)(2,1)} %facets_ref.1, s32[1,4]{1,0:T(1,128)} %sub_hbm.1, s32[1]{0:T(128)S(6)} %copy.7.col_ref, s32[1,1]{1,0:T(1,128)S(6)} %copy.8.pick_ref), custom_call_target="tpu_custom_call" | custom-call | tf_op jit(solution)/shard_map/send/pallas_call | solution.py:461
  2.8 7.3 %all-to-all-start = ((bf16[32,8,384]{2,1,0:T(8,128)(2,1)}), bf16[32,8,384]{2,1,0:T(8,128)(2,1)S(1)}, u32[]{:S(2)}, u32[]{:S(2)}) async-start(bf16[32,8,384]{2,1,0:T(8,128)(2,1)} %send.1), calls=%async_computation | async-start | bytes 393216 | tf_op jit(solution)/shard_map/all_to_all | solution.py:474
  10.2 1.6 %tables.1 = (bf16[4,256,256]{2,1,0:T(8,128)(2,1)S(1)}, bf16[512,256]{1,0:T(8,128)(2,1)S(1)}, bf16[256,512]{1,0:T(8,128)(2,1)S(1)}, bf16[32,256]{1,0:T(8,128)(2,1...) custom-call(f32[4,2,256,256]{3,2,1,0:T(8,128)} %screens_hbm.1), custom_call_target="tpu_custom_call" | custom-call | flops 329318400 | bytes 6586368 | tf_op jit(solution)/shard_map/tables/pallas_call | solution.py:486
  11.8 7.3 %all-to-all-done = bf16[32,8,384]{2,1,0:T(8,128)(2,1)S(1)} async-done(((bf16[32,8,384]{2,1,0:T(8,128)(2,1)}), bf16[32,8,384]{2,1,0:T(8,128)(2,1)S(1)}, u32[]{:S(2)}, u32[]{:S(2)}) %all-to-all-start) | async-done | bytes 196640 | tf_op jit(solution)/shard_map/all_to_all | solution.py:474
  19.1 5.2 %window.1 = (f32[8,256]{1,0:T(8,128)S(1)}, f32[8,256]{1,0:T(8,128)S(1)}) custom-call(bf16[256,384]{1,0:T(8,128)(2,1)S(1)} %bitcast.3, bf16[4,256,256]{2,1,0:T(8,128)(2,1)S(1)} %get-tuple-element.13.a_ref, bf16[512,256]{1,0:T(8,128)(2,1)S(1)} %get-tuple-element.14.wp_ref, bf16[256,512]{1,0:T(8,128)(2,1)S(1)} %get-tuple-element.15.wt_ref, ...), custom_call_target="tpu_custom_call" | custom-call | tf_op jit(solution)/shard_map/window/pallas_call | solution.py:498
  24.3 0.6 %collective-permute-start = (f32[8,256]{1,0:T(8,128)S(1)}, f32[8,256]{1,0:T(8,128)S(1)}, u32[]{:S(2)}, u32[]{:S(2)}) collective-permute-start(f32[8,256]{1,0:T(8,128)S(1)} %get-tuple-element.20), channel_id=1, source_target_pairs={{0,1},{1,0},{2,3},{3,2},{4,5},{5,4},{6,7},{7,6},{8,9},{9,8},{10,11... | collective-permute-start | bytes 24584 | tf_op jit(solution)/shard_map/ppermute | solution.py:519
  24.9 0.8 %collective-permute-done = f32[8,256]{1,0:T(8,128)S(1)} collective-permute-done((f32[8,256]{1,0:T(8,128)S(1)}, f32[8,256]{1,0:T(8,128)S(1)}, u32[]{:S(2)}, u32[]{:S(2)}) %collective-permute-start) | collective-permute-done | bytes 8224 | tf_op jit(solution)/shard_map/ppermute | solution.py:519
  25.7 0.6 %copy.6 = f32[1,8,2,128]{3,2,1,0:T(2,128)} copy(f32[1,8,2,128]{3,1,2,0:T(8,128)S(1)} %multiply_bitcast_fusion) | data formatting | bytes 16384 | tf_op jit(solution)/shard_map/reshape | solution.py:520
  (1 shorter events, 0.0 us)
Async XLA Ops:
  2.8 16.3 %all-to-all-start = ((bf16[32,8,384]{2,1,0:T(8,128)(2,1)}), bf16[32,8,384]{2,1,0:T(8,128)(2,1)S(1)}, u32[]{:S(2)}, u32[]{:S(2)}) async-start(bf16[32,8,384]{2,1,0:T(8,128)(2,1)} %send.1), calls=%async_computation | async-start | bytes 393216 | tf_op jit(solution)/shard_map/all_to_all | solution.py:474
  24.3 1.4 %collective-permute-start = (f32[8,256]{1,0:T(8,128)S(1)}, f32[8,256]{1,0:T(8,128)S(1)}, u32[]{:S(2)}, u32[]{:S(2)}) collective-permute-start(f32[8,256]{1,0:T(8,128)S(1)} %get-tuple-element.20), channel_id=1, source_target_pairs={{0,1},{1,0},{2,3},{3,2},{4,5},{5,4},{6,7},{7,6},{8,9},{9,8},{10,11... | collective-permute-start | bytes 24584 | tf_op jit(solution)/shard_map/ppermute | solution.py:519

commit v6 on v5

--- a/solution.py
+++ b/solution.py
@@ -247,14 +247,13 @@
     for copy in copies:
         copy.wait()
     numbers = (col_ref[0], sub_ref[0, lax.axis_index("facet")], pick_ref[0, 0])
-    lane = iota((facets_ref.shape[1], LANES), 1)
-    told = jnp.zeros(lane.shape, jnp.int32)
+    shape = (1, 2, out_ref.shape[3])
+    lane, low = iota(shape, 2), iota(shape, 1) == 1
+    told = jnp.zeros(shape, jnp.int32)
     for i, number in enumerate(numbers):
-        told = jnp.where(lane == i, number >> HALF, told)
-        told = jnp.where(lane == i + len(numbers), number & ((1 << HALF) - 1), told)
-    mine = jnp.concatenate(
-        [mine_ref[0, :, 0, :], mine_ref[0, :, 1, :], told.astype(F32).astype(BF16)], axis=1
-    )
+        value = jnp.where(low, number & ((1 << HALF) - 1), number >> HALF)
+        told = jnp.where(lane == i, value, told)
+    mine = jnp.concatenate([mine_ref[0], told.astype(F32).astype(BF16)], axis=0)
     out_ref[...] = jnp.broadcast_to(mine[None], out_ref.shape)
 
 
@@ -326,7 +325,7 @@
 
 def pair_kernel(
     dims, x_ref, a_ref, wp_ref, wt_ref, low_ref, wa_ref, screens_ref, mine_ref, other_ref,
-    told_ref, numbers_ref, spread_ref, down_ref, half_ref, lifted_ref, seen_ref, gathered_ref, phase_ref, sem,
+    wide_ref, told_ref, numbers_ref, spread_ref, down_ref, half_ref, lifted_ref, seen_ref, gathered_ref, phase_ref, sem,
 ):
     facets, height, span, slab, size, columns, local = dims
     rows = facets * height
@@ -336,17 +335,26 @@
     core = lax.axis_index("col") & 1
     base = lax.axis_index("facet") * height + (lax.axis_index("col") >> 1) * pair_rows
 
-    lane, line = iota((ROWS, LANES), 1), iota((ROWS, LANES), 0)
-    weights = jnp.where(lane == line, 1 << HALF, jnp.where(lane == line + 3, 1, 0))
-    weights = jnp.where(line < 3, weights, 0).astype(F32).astype(BF16)
-    told = dot_nt(weights, x_ref[:, 2 * slab :])
-    told_ref[...] = told.astype(jnp.int32)
+    pitch = 2 * (local + 1)
+    devices = x_ref.shape[0] // pitch
+    wide_ref[...] = x_ref[...].astype(F32)
+    told = [
+        jnp.concatenate(
+            [wide_ref[k * pitch + 2 * local + h : k * pitch + 2 * local + h + 1] for k in range(devices)],
+            axis=0,
+        )
+        for h in (0, 1)
+    ]
+    told_ref[...] = (told[0] * (1 << HALF) + told[1]).astype(jnp.int32)
     copy = pltpu.make_async_copy(told_ref, numbers_ref, sem)
     copy.start()
-    copy.wait()
 
     def number(kind, facet, column):
-        return numbers_ref[kind, (facet * columns + column) * local]
+        return numbers_ref[facet * columns + column, kind]
+
+    def spread_number(kind, facet, column, shape):
+        own = told_ref[pl.ds(facet * columns + column, 1), :]
+        return jnp.broadcast_to(own[:, kind : kind + 1], shape)
 
     def times(a, b):
         return a[0] * b[0] - a[1] * b[1], a[0] * b[1] + a[1] * b[0]
@@ -355,21 +363,26 @@
         real, imag = wave((where * offset) & (NPAD - 1), NPAD, 1.0)
         return real, -imag
 
+    own = [
+        jnp.concatenate(
+            [wide_ref[pl.ds(k * pitch + h, local, stride=2), :] for k in range(devices)], axis=0
+        )
+        for h in (0, 1)
+    ]
     for i in range(mine_columns):
         column = 2 * i + core
-        ahead = phases(number(0, 0, column), iota((ROWS, slab), 1))
+        ahead = phases(spread_number(0, 0, column, (ROWS, slab)), iota((ROWS, slab), 1))
         phase_ref[2 * i * ROWS : (2 * i + 1) * ROWS, :] = ahead[0]
         phase_ref[(2 * i + 1) * ROWS : (2 * i + 2) * ROWS, :] = ahead[1]
         line = iota((ROWS, rows), 0)
         offset_rows = jnp.zeros((ROWS, rows), jnp.int32)
         for s in range(subgrids):
-            offset_rows = jnp.where(line == s, number(1, s, column), offset_rows)
+            offset_rows = jnp.where(line == s, spread_number(1, s, column, line.shape), offset_rows)
         row_phase = phases(offset_rows, iota((ROWS, rows), 1))
         for h in (0, 1):
             down_ref[i, h, :, :ROWS] = row_phase[h].T
-        own = x_ref[:, : 2 * slab].astype(F32)
         real, imag = times(
-            (own[:, :slab], own[:, slab:]),
+            own,
             [jnp.broadcast_to(p[:1], (rows, slab)) for p in ahead],
         )
         turned = jnp.concatenate([real.astype(BF16), imag.astype(BF16)], axis=1)
@@ -422,6 +435,7 @@
         gathered_ref[part, size:] = sums[1].astype(BF16)
 
     lift(0, 0)
+    copy.wait()
     for i in range(mine_columns):
         one_column(i, i % 2, i + 1 if i + 1 < mine_columns else None)
 
@@ -456,11 +470,10 @@
     dims = (facet_count, height, span, slab, size, column_count, local_rows)
     any_space = pl.BlockSpec(memory_space=pl.ANY)
     smem = pl.BlockSpec(memory_space=pltpu.MemorySpace.SMEM)
-    width = 2 * slab + LANES
 
     outgoing = pl.pallas_call(
         pair_send_kernel,
-        out_shape=jax.ShapeDtypeStruct((devices, local_rows, width), BF16),
+        out_shape=jax.ShapeDtypeStruct((devices, local_rows + 1, 2, slab), BF16),
         in_specs=[any_space, any_space, smem, smem],
         out_specs=pl.BlockSpec(memory_space=VMEM),
         scratch_shapes=[
@@ -473,7 +486,7 @@
     )(in_hbm(facets), in_hbm(sub_offsets), col_offsets, screen_index)
     everyone = lax.all_to_all(
         outgoing, ("facet", "col"), split_axis=0, concat_axis=0, tiled=True
-    ).reshape(rows, width)
+    ).reshape(devices * (local_rows + 1) * 2, slab)
     table_shapes = [
         ((facet_count, 2 * span, 2 * slab), BF16),
         ((2 * size, rows), BF16),
@@ -501,8 +514,9 @@
         in_specs=whole(1 + len(tables)),
         out_specs=whole(2),
         scratch_shapes=[
-            pltpu.VMEM((ROWS, rows), jnp.int32),
-            pltpu.SMEM((ROWS, rows), jnp.int32),
+            pltpu.VMEM(everyone.shape, F32),
+            pltpu.VMEM((devices, slab), jnp.int32),
+            pltpu.SMEM((devices, slab), jnp.int32),
             pltpu.VMEM((column_count // 2, rows, 2 * span), F32),
             pltpu.VMEM((column_count // 2, 2, rows, LANES), F32),
             pltpu.VMEM((2, subgrid_count * size, 2 * span), BF16),

time: 26.6 us -> 25.5 us (0.959)
  waiting for transfers between devices: 8.16 us -> 7.7 us
  Pallas kernels: 8.3 us -> 7.92 us
    all_to_all x1, waiting for transfers between devices: 7.33 us -> 6.79 us  [pair_body(): lax.all_to_all(outgoing, ('facet', 'col'), split_axis=0, concat_axis=0, t...]
    pallas_call x1, Pallas kernels: 5.17 us -> 4.77 us  [pair_body(): pl.pallas_call(functools.partial(pair_kernel, dims), out_shape=[jax.Shape...]
where the time goes in v6:
time: 25.5 us; the launch traced here: 25.2 us
  Pallas kernels  7.92 us (31%)
  waiting for transfers between devices  7.7 us (30%)
  starting transfers between devices  7.66 us (30%)
  between operations  1.33 us (5%)
  local copies, waits for them, and re-layouts  0.61 us (2%)
    all_to_all x1, starting transfers between devices, pair_body(): lax.all_to_all(outgoing, ('facet', 'col'), split_axis=0, concat_axis=0, t...  7.33 us
    all_to_all x1, waiting for transfers between devices, pair_body(): lax.all_to_all(outgoing, ('facet', 'col'), split_axis=0, concat_axis=0, t...  6.79 us
    pallas_call x1, Pallas kernels, pair_body(): pl.pallas_call(functools.partial(pair_kernel, dims), out_shape=[jax.Shape...  4.77 us
    pallas_call x1, Pallas kernels, pair_body(): pl.pallas_call(functools.partial(pair_tables_kernel, dims), out_shape=[ja...  1.61 us
    pallas_call x1, Pallas kernels, pair_body(): pl.pallas_call(pair_send_kernel, out_shape=jax.ShapeDtypeStruct((devices,...  1.54 us
    ppermute x1, waiting for transfers between devices, pair_body(): summed = mine + lax.ppermute(other, 'col', swap)  0.91 us
    reshape x1, local copies, waits for them, and re-layouts, pair_body(): (summed / math.sqrt(column_count * subgrid_count)).reshape(1, local_rows,...  0.61 us
  transfers between devices with their start and end apart: 2, of which 2 were waited for; matrix products, arithmetic and copies ran while one was open for 0% of the time, Pallas kernels for 6%

profile of v6, /device:TPU:0, one launch (start us, length us, event | category | flops | bytes accessed | tf_op | source)
XLA Modules:
  0.0 25.2 jit_solution(3111697166530422534)
XLA Ops:
  1.3 1.5 %send.1 = bf16[32,9,2,128]{3,2,1,0:T(2,128)(2,1)} custom-call(bf16[1,8,2,128]{3,2,1,0:T(2,128)(2,1)} %facets_ref.1, s32[1,4]{1,0:T(1,128)} %sub_hbm.1, s32[1]{0:T(128)S(6)} %copy.7.col_ref, s32[1,1]{1,0:T(1,128)S(6)} %copy.8.pick_ref), custom_call_target="tpu_custom_call" | custom-call | tf_op jit(solution)/shard_map/send/pallas_call | solution.py:474
  2.8 7.3 %all-to-all-start = ((bf16[32,9,2,128]{3,2,1,0:T(2,128)(2,1)}), bf16[32,9,2,128]{3,2,1,0:T(2,128)(2,1)S(1)}, u32[]{:S(2)}, u32[]{:S(2)}) async-start(bf16[32,9,2,128]{3,2,1,0:T(2,128)(2,1)} %send.1), calls=%async_computation | async-start | bytes 294912 | tf_op jit(solution)/shard_map/all_to_all | solution.py:487
  10.2 1.6 %tables.1 = (bf16[4,256,256]{2,1,0:T(8,128)(2,1)S(1)}, bf16[512,256]{1,0:T(8,128)(2,1)S(1)}, bf16[256,512]{1,0:T(8,128)(2,1)S(1)}, bf16[32,256]{1,0:T(8,128)(2,1...) custom-call(f32[4,2,256,256]{3,2,1,0:T(8,128)} %screens_hbm.1), custom_call_target="tpu_custom_call" | custom-call | flops 329318400 | bytes 6586368 | tf_op jit(solution)/shard_map/tables/pallas_call | solution.py:499
  11.8 6.8 %all-to-all-done = bf16[32,9,2,128]{3,2,1,0:T(2,128)(2,1)S(1)} async-done(((bf16[32,9,2,128]{3,2,1,0:T(2,128)(2,1)}), bf16[32,9,2,128]{3,2,1,0:T(2,128)(2,1)S(1)}, u32[]{:S(2)}, u32[]{:S(2)}) %all-to-all-start) | async-done | bytes 147488 | tf_op jit(solution)/shard_map/all_to_all | solution.py:487
  18.6 4.8 %window.1 = (f32[8,256]{1,0:T(8,128)S(1)}, f32[8,256]{1,0:T(8,128)S(1)}) custom-call(bf16[576,128]{1,0:T(8,128)(2,1)S(1)} %bitcast.3, bf16[4,256,256]{2,1,0:T(8,128)(2,1)S(1)} %get-tuple-element.13.a_ref, bf16[512,256]{1,0:T(8,128)(2,1)S(1)} %get-tuple-element.14.wp_ref, bf16[256,512]{1,0:T(8,128)(2,1)S(1)} %get-tuple-element.15.wt_ref, ...), custom_call_target="tpu_custom_call" | custom-call | tf_op jit(solution)/shard_map/window/pallas_call | solution.py:511
  23.4 0.3 %collective-permute-start = (f32[8,256]{1,0:T(8,128)S(1)}, f32[8,256]{1,0:T(8,128)S(1)}, u32[]{:S(2)}, u32[]{:S(2)}) collective-permute-start(f32[8,256]{1,0:T(8,128)S(1)} %get-tuple-element.20), channel_id=1, source_target_pairs={{0,1},{1,0},{2,3},{3,2},{4,5},{5,4},{6,7},{7,6},{8,9},{9,8},{10,11... | collective-permute-start | bytes 24584 | tf_op jit(solution)/shard_map/ppermute | solution.py:533
  23.7 0.9 %collective-permute-done = f32[8,256]{1,0:T(8,128)S(1)} collective-permute-done((f32[8,256]{1,0:T(8,128)S(1)}, f32[8,256]{1,0:T(8,128)S(1)}, u32[]{:S(2)}, u32[]{:S(2)}) %collective-permute-start) | collective-permute-done | bytes 8224 | tf_op jit(solution)/shard_map/ppermute | solution.py:533
  24.6 0.6 %copy.6 = f32[1,8,2,128]{3,2,1,0:T(2,128)} copy(f32[1,8,2,128]{3,1,2,0:T(8,128)S(1)} %multiply_bitcast_fusion) | data formatting | bytes 16384 | tf_op jit(solution)/shard_map/reshape | solution.py:534
  (1 shorter events, 0.0 us)
Async XLA Ops:
  2.8 15.8 %all-to-all-start = ((bf16[32,9,2,128]{3,2,1,0:T(2,128)(2,1)}), bf16[32,9,2,128]{3,2,1,0:T(2,128)(2,1)S(1)}, u32[]{:S(2)}, u32[]{:S(2)}) async-start(bf16[32,9,2,128]{3,2,1,0:T(2,128)(2,1)} %send.1), calls=%async_computation | async-start | bytes 294912 | tf_op jit(solution)/shard_map/all_to_all | solution.py:487
  23.4 1.2 %collective-permute-start = (f32[8,256]{1,0:T(8,128)S(1)}, f32[8,256]{1,0:T(8,128)S(1)}, u32[]{:S(2)}, u32[]{:S(2)}) collective-permute-start(f32[8,256]{1,0:T(8,128)S(1)} %get-tuple-element.20), channel_id=1, source_target_pairs={{0,1},{1,0},{2,3},{3,2},{4,5},{5,4},{6,7},{7,6},{8,9},{9,8},{10,11... | collective-permute-start | bytes 24584 | tf_op jit(solution)/shard_map/ppermute | solution.py:533

commit v7 on v6

--- a/solution.py
+++ b/solution.py
@@ -15,7 +15,6 @@
 LANES = 128
 CHUNK = 256
 HALF = 7
-UNROLL = False
 VMEM_LIMIT = 24 * 2**20
 F32 = jnp.float32
 BF16 = jnp.bfloat16
@@ -397,7 +396,7 @@
             lifted_ref[slot, s, :, :span] = real.astype(BF16)
             lifted_ref[slot, s, :, span:] = imag.astype(BF16)
 
-    def one_column(i, slot, following):
+    def halve(slot):
         for s in range(subgrids):
             lifted = lifted_ref[slot, s]
             first = dot(wp_ref[:size], lifted)
@@ -405,8 +404,12 @@
             part = slice(s * size, (s + 1) * size)
             half_ref[slot, part, :span] = (first[:, :span] - second[:, span:]).astype(BF16)
             half_ref[slot, part, span:] = (first[:, span:] + second[:, :span]).astype(BF16)
+
+    def one_column(i, slot, following):
         if following is not None:
-            lift(following, 1 - slot)
+            halve(1 - slot)
+        if following is not None and following + 1 < mine_columns:
+            lift(following + 1, slot)
         half = half_ref[slot]
         all_real, all_imag = dot(half, wt_ref[:, :size]), dot(half, wt_ref[:, size:])
         for s in range(subgrids):
@@ -435,6 +438,8 @@
         gathered_ref[part, size:] = sums[1].astype(BF16)
 
     lift(0, 0)
+    halve(0)
+    lift(1, 1)
     copy.wait()
     for i in range(mine_columns):
         one_column(i, i % 2, i + 1 if i + 1 < mine_columns else None)
@@ -621,7 +626,7 @@
 
 def body(facets, sub_offsets, col_offsets, screen_index, screens):
     columns, subgrids = lax.axis_size("col"), sub_offsets.shape[1]
-    alone = columns % 2 == 0 and subgrids == lax.axis_size("facet") and columns * subgrids <= 32
+    alone = columns % 4 == 0 and subgrids == lax.axis_size("facet") and columns * subgrids <= 32
     run = pair_body if alone else spread_body
     return run(facets, sub_offsets, col_offsets, screen_index, screens)
 

time: 25.5 us -> 25.3 us (level)
  no operation moved by 1% of the time
where the time goes in v7:
time: 25.3 us; the launch traced here: 25 us
  Pallas kernels  7.73 us (31%)
  waiting for transfers between devices  7.7 us (30%)
  starting transfers between devices  7.66 us (30%)
  between operations  1.33 us (5%)
  local copies, waits for them, and re-layouts  0.61 us (2%)
    all_to_all x1, starting transfers between devices, pair_body(): lax.all_to_all(outgoing, ('facet', 'col'), split_axis=0, concat_axis=0, t...  7.33 us
    all_to_all x1, waiting for transfers between devices, pair_body(): lax.all_to_all(outgoing, ('facet', 'col'), split_axis=0, concat_axis=0, t...  6.79 us
    pallas_call x1, Pallas kernels, pair_body(): pl.pallas_call(functools.partial(pair_kernel, dims), out_shape=[jax.Shape...  4.58 us
    pallas_call x1, Pallas kernels, pair_body(): pl.pallas_call(functools.partial(pair_tables_kernel, dims), out_shape=[ja...  1.61 us
    pallas_call x1, Pallas kernels, pair_body(): pl.pallas_call(pair_send_kernel, out_shape=jax.ShapeDtypeStruct((devices,...  1.54 us
    ppermute x1, waiting for transfers between devices, pair_body(): summed = mine + lax.ppermute(other, 'col', swap)  0.91 us
    reshape x1, local copies, waits for them, and re-layouts, pair_body(): (summed / math.sqrt(column_count * subgrid_count)).reshape(1, local_rows,...  0.61 us
  transfers between devices with their start and end apart: 2, of which 2 were waited for; matrix products, arithmetic and copies ran while one was open for 0% of the time, Pallas kernels for 6%

profile of v7, /device:TPU:0, one launch (start us, length us, event | category | flops | bytes accessed | tf_op | source)
XLA Modules:
  0.0 25.0 jit_solution(2486154815447223272)
XLA Ops:
  1.3 1.5 %send.1 = bf16[32,9,2,128]{3,2,1,0:T(2,128)(2,1)} custom-call(bf16[1,8,2,128]{3,2,1,0:T(2,128)(2,1)} %facets_ref.1, s32[1,4]{1,0:T(1,128)} %sub_hbm.1, s32[1]{0:T(128)S(6)} %copy.7.col_ref, s32[1,1]{1,0:T(1,128)S(6)} %copy.8.pick_ref), custom_call_target="tpu_custom_call" | custom-call | tf_op jit(solution)/shard_map/send/pallas_call | solution.py:479
  2.8 7.3 %all-to-all-start = ((bf16[32,9,2,128]{3,2,1,0:T(2,128)(2,1)}), bf16[32,9,2,128]{3,2,1,0:T(2,128)(2,1)S(1)}, u32[]{:S(2)}, u32[]{:S(2)}) async-start(bf16[32,9,2,128]{3,2,1,0:T(2,128)(2,1)} %send.1), calls=%async_computation | async-start | bytes 294912 | tf_op jit(solution)/shard_map/all_to_all | solution.py:492
  10.2 1.6 %tables.1 = (bf16[4,256,256]{2,1,0:T(8,128)(2,1)S(1)}, bf16[512,256]{1,0:T(8,128)(2,1)S(1)}, bf16[256,512]{1,0:T(8,128)(2,1)S(1)}, bf16[32,256]{1,0:T(8,128)(2,1...) custom-call(f32[4,2,256,256]{3,2,1,0:T(8,128)} %screens_hbm.1), custom_call_target="tpu_custom_call" | custom-call | flops 329318400 | bytes 6586368 | tf_op jit(solution)/shard_map/tables/pallas_call | solution.py:504
  11.8 6.8 %all-to-all-done = bf16[32,9,2,128]{3,2,1,0:T(2,128)(2,1)S(1)} async-done(((bf16[32,9,2,128]{3,2,1,0:T(2,128)(2,1)}), bf16[32,9,2,128]{3,2,1,0:T(2,128)(2,1)S(1)}, u32[]{:S(2)}, u32[]{:S(2)}) %all-to-all-start) | async-done | bytes 147488 | tf_op jit(solution)/shard_map/all_to_all | solution.py:492
  18.6 4.6 %window.1 = (f32[8,256]{1,0:T(8,128)S(1)}, f32[8,256]{1,0:T(8,128)S(1)}) custom-call(bf16[576,128]{1,0:T(8,128)(2,1)S(1)} %bitcast.3, bf16[4,256,256]{2,1,0:T(8,128)(2,1)S(1)} %get-tuple-element.13.a_ref, bf16[512,256]{1,0:T(8,128)(2,1)S(1)} %get-tuple-element.14.wp_ref, bf16[256,512]{1,0:T(8,128)(2,1)S(1)} %get-tuple-element.15.wt_ref, ...), custom_call_target="tpu_custom_call" | custom-call | tf_op jit(solution)/shard_map/window/pallas_call | solution.py:516
  23.2 0.3 %collective-permute-start = (f32[8,256]{1,0:T(8,128)S(1)}, f32[8,256]{1,0:T(8,128)S(1)}, u32[]{:S(2)}, u32[]{:S(2)}) collective-permute-start(f32[8,256]{1,0:T(8,128)S(1)} %get-tuple-element.20), channel_id=1, source_target_pairs={{0,1},{1,0},{2,3},{3,2},{4,5},{5,4},{6,7},{7,6},{8,9},{9,8},{10,11... | collective-permute-start | bytes 24584 | tf_op jit(solution)/shard_map/ppermute | solution.py:538
  23.5 0.9 %collective-permute-done = f32[8,256]{1,0:T(8,128)S(1)} collective-permute-done((f32[8,256]{1,0:T(8,128)S(1)}, f32[8,256]{1,0:T(8,128)S(1)}, u32[]{:S(2)}, u32[]{:S(2)}) %collective-permute-start) | collective-permute-done | bytes 8224 | tf_op jit(solution)/shard_map/ppermute | solution.py:538
  24.4 0.6 %copy.6 = f32[1,8,2,128]{3,2,1,0:T(2,128)} copy(f32[1,8,2,128]{3,1,2,0:T(8,128)S(1)} %multiply_bitcast_fusion) | data formatting | bytes 16384 | tf_op jit(solution)/shard_map/reshape | solution.py:539
  (1 shorter events, 0.0 us)
Async XLA Ops:
  2.8 15.8 %all-to-all-start = ((bf16[32,9,2,128]{3,2,1,0:T(2,128)(2,1)}), bf16[32,9,2,128]{3,2,1,0:T(2,128)(2,1)S(1)}, u32[]{:S(2)}, u32[]{:S(2)}) async-start(bf16[32,9,2,128]{3,2,1,0:T(2,128)(2,1)} %send.1), calls=%async_computation | async-start | bytes 294912 | tf_op jit(solution)/shard_map/all_to_all | solution.py:492
  23.2 1.2 %collective-permute-start = (f32[8,256]{1,0:T(8,128)S(1)}, f32[8,256]{1,0:T(8,128)S(1)}, u32[]{:S(2)}, u32[]{:S(2)}) collective-permute-start(f32[8,256]{1,0:T(8,128)S(1)} %get-tuple-element.20), channel_id=1, source_target_pairs={{0,1},{1,0},{2,3},{3,2},{4,5},{5,4},{6,7},{7,6},{8,9},{9,8},{10,11... | collective-permute-start | bytes 24584 | tf_op jit(solution)/shard_map/ppermute | solution.py:538

commit v8 on v7

--- a/solution.py
+++ b/solution.py
@@ -384,10 +384,12 @@
             own,
             [jnp.broadcast_to(p[:1], (rows, slab)) for p in ahead],
         )
-        turned = jnp.concatenate([real.astype(BF16), imag.astype(BF16)], axis=1)
+        both = jnp.concatenate([real, imag], axis=1)
+        turned = both.astype(BF16)
+        rest = (both - turned.astype(F32)).astype(BF16)
         for f in range(facets):
             part = slice(f * height, (f + 1) * height)
-            spread_ref[i, part, :] = dot(turned[part], a_ref[f])
+            spread_ref[i, part, :] = dot(turned[part], a_ref[f]) + dot(rest[part], a_ref[f])
 
     def lift(i, slot):
         for s in range(subgrids):

time: 25.3 us -> 25.3 us (level)
  no operation moved by 1% of the time
where the time goes in v8:
time: 25.3 us; the launch traced here: 25.1 us
  Pallas kernels  7.76 us (31%)
  waiting for transfers between devices  7.69 us (30%)
  starting transfers between devices  7.67 us (30%)
  between operations  1.33 us (5%)
  local copies, waits for them, and re-layouts  0.61 us (2%)
    all_to_all x1, starting transfers between devices, pair_body(): lax.all_to_all(outgoing, ('facet', 'col'), split_axis=0, concat_axis=0, t...  7.33 us
    all_to_all x1, waiting for transfers between devices, pair_body(): lax.all_to_all(outgoing, ('facet', 'col'), split_axis=0, concat_axis=0, t...  6.79 us
    pallas_call x1, Pallas kernels, pair_body(): pl.pallas_call(functools.partial(pair_kernel, dims), out_shape=[jax.Shape...  4.61 us
    pallas_call x1, Pallas kernels, pair_body(): pl.pallas_call(functools.partial(pair_tables_kernel, dims), out_shape=[ja...  1.61 us
    pallas_call x1, Pallas kernels, pair_body(): pl.pallas_call(pair_send_kernel, out_shape=jax.ShapeDtypeStruct((devices,...  1.54 us
    ppermute x1, waiting for transfers between devices, pair_body(): summed = mine + lax.ppermute(other, 'col', swap)  0.9 us
    reshape x1, local copies, waits for them, and re-layouts, pair_body(): (summed / math.sqrt(column_count * subgrid_count)).reshape(1, local_rows,...  0.61 us
  transfers between devices with their start and end apart: 2, of which 2 were waited for; matrix products, arithmetic and copies ran while one was open for 0% of the time, Pallas kernels for 6%

profile of v8, /device:TPU:0, one launch (start us, length us, event | category | flops | bytes accessed | tf_op | source)
XLA Modules:
  0.0 25.1 jit_solution(7730537982039012389)
XLA Ops:
  1.3 1.5 %send.1 = bf16[32,9,2,128]{3,2,1,0:T(2,128)(2,1)} custom-call(bf16[1,8,2,128]{3,2,1,0:T(2,128)(2,1)} %facets_ref.1, s32[1,4]{1,0:T(1,128)} %sub_hbm.1, s32[1]{0:T(128)S(6)} %copy.7.col_ref, s32[1,1]{1,0:T(1,128)S(6)} %copy.8.pick_ref), custom_call_target="tpu_custom_call" | custom-call | tf_op jit(solution)/shard_map/send/pallas_call | solution.py:481
  2.8 7.3 %all-to-all-start = ((bf16[32,9,2,128]{3,2,1,0:T(2,128)(2,1)}), bf16[32,9,2,128]{3,2,1,0:T(2,128)(2,1)S(1)}, u32[]{:S(2)}, u32[]{:S(2)}) async-start(bf16[32,9,2,128]{3,2,1,0:T(2,128)(2,1)} %send.1), calls=%async_computation | async-start | bytes 294912 | tf_op jit(solution)/shard_map/all_to_all | solution.py:494
  10.2 1.6 %tables.1 = (bf16[4,256,256]{2,1,0:T(8,128)(2,1)S(1)}, bf16[512,256]{1,0:T(8,128)(2,1)S(1)}, bf16[256,512]{1,0:T(8,128)(2,1)S(1)}, bf16[32,256]{1,0:T(8,128)(2,1...) custom-call(f32[4,2,256,256]{3,2,1,0:T(8,128)} %screens_hbm.1), custom_call_target="tpu_custom_call" | custom-call | flops 329318400 | bytes 6586368 | tf_op jit(solution)/shard_map/tables/pallas_call | solution.py:506
  11.8 6.8 %all-to-all-done = bf16[32,9,2,128]{3,2,1,0:T(2,128)(2,1)S(1)} async-done(((bf16[32,9,2,128]{3,2,1,0:T(2,128)(2,1)}), bf16[32,9,2,128]{3,2,1,0:T(2,128)(2,1)S(1)}, u32[]{:S(2)}, u32[]{:S(2)}) %all-to-all-start) | async-done | bytes 147488 | tf_op jit(solution)/shard_map/all_to_all | solution.py:494
  18.6 4.6 %window.1 = (f32[8,256]{1,0:T(8,128)S(1)}, f32[8,256]{1,0:T(8,128)S(1)}) custom-call(bf16[576,128]{1,0:T(8,128)(2,1)S(1)} %bitcast.3, bf16[4,256,256]{2,1,0:T(8,128)(2,1)S(1)} %get-tuple-element.13.a_ref, bf16[512,256]{1,0:T(8,128)(2,1)S(1)} %get-tuple-element.14.wp_ref, bf16[256,512]{1,0:T(8,128)(2,1)S(1)} %get-tuple-element.15.wt_ref, ...), custom_call_target="tpu_custom_call" | custom-call | tf_op jit(solution)/shard_map/window/pallas_call | solution.py:518
  23.2 0.3 %collective-permute-start = (f32[8,256]{1,0:T(8,128)S(1)}, f32[8,256]{1,0:T(8,128)S(1)}, u32[]{:S(2)}, u32[]{:S(2)}) collective-permute-start(f32[8,256]{1,0:T(8,128)S(1)} %get-tuple-element.20), channel_id=1, source_target_pairs={{0,1},{1,0},{2,3},{3,2},{4,5},{5,4},{6,7},{7,6},{8,9},{9,8},{10,11... | collective-permute-start | bytes 24584 | tf_op jit(solution)/shard_map/ppermute | solution.py:540
  23.6 0.9 %collective-permute-done = f32[8,256]{1,0:T(8,128)S(1)} collective-permute-done((f32[8,256]{1,0:T(8,128)S(1)}, f32[8,256]{1,0:T(8,128)S(1)}, u32[]{:S(2)}, u32[]{:S(2)}) %collective-permute-start) | collective-permute-done | bytes 8224 | tf_op jit(solution)/shard_map/ppermute | solution.py:540
  24.5 0.6 %copy.6 = f32[1,8,2,128]{3,2,1,0:T(2,128)} copy(f32[1,8,2,128]{3,1,2,0:T(8,128)S(1)} %multiply_bitcast_fusion) | data formatting | bytes 16384 | tf_op jit(solution)/shard_map/reshape | solution.py:541
  (1 shorter events, 0.0 us)
Async XLA Ops:
  2.8 15.8 %all-to-all-start = ((bf16[32,9,2,128]{3,2,1,0:T(2,128)(2,1)}), bf16[32,9,2,128]{3,2,1,0:T(2,128)(2,1)S(1)}, u32[]{:S(2)}, u32[]{:S(2)}) async-start(bf16[32,9,2,128]{3,2,1,0:T(2,128)(2,1)} %send.1), calls=%async_computation | async-start | bytes 294912 | tf_op jit(solution)/shard_map/all_to_all | solution.py:494
  23.2 1.2 %collective-permute-start = (f32[8,256]{1,0:T(8,128)S(1)}, f32[8,256]{1,0:T(8,128)S(1)}, u32[]{:S(2)}, u32[]{:S(2)}) collective-permute-start(f32[8,256]{1,0:T(8,128)S(1)} %get-tuple-element.20), channel_id=1, source_target_pairs={{0,1},{1,0},{2,3},{3,2},{4,5},{5,4},{6,7},{7,6},{8,9},{9,8},{10,11... | collective-permute-start | bytes 24584 | tf_op jit(solution)/shard_map/ppermute | solution.py:540
